TPU v7x, 128 devices: a whole 4x4x4 slice. The times are simulated.
128 devices in a mesh: clip: 2 (over core), tm: 16 (over z, x), head: 4 (over y).
Axes of the slice: x: 4, y: 4, z: 4, core: 2. Of those that a mesh axis runs over, the one named last changes fastest.
Arguments:
- video_tokens: bfloat16 [64, 1568, 1024], P(('clip', 'tm')), parts along dimension 0, may hold values from -6 to 6
- window_order: int32 [64, 1568], P(('clip', 'tm')), parts along dimension 0, may hold values from 0 to 1567, each once within a row
- clip_id: int32 [64], P(('clip', 'tm')), parts along dimension 0, may hold values from 0 to 7, never falling along the last dimension, each value on 1 to 8 neighbouring positions
- attend_weight: bfloat16 [3, 1024, 1024], P(None, None, 'head'), may hold values from -0.75 to 0.75
- attend_out: bfloat16 [1024, 1024], P('head'), may hold values from -0.1875 to 0.1875
- recur_weight: bfloat16 [3, 1024, 1024], P(None, None, 'head'), may hold values from -0.1875 to 0.1875
- frame_decay: float32 [64, 1024], P(('clip', 'tm'), 'head'), parts along dimension 0, may hold values from -5.7 to -0.010625, as said below
- recur_out: bfloat16 [1024, 1024], P('head'), may hold values from -0.1875 to 0.1875
Outputs:
- features_out: bfloat16 [64, 1568, 1024], P(('clip', 'tm'), None, 'head'), parts along dimension 0
There are 2 independent parts, one for each index of `clip`. A program takes and returns all parts, laid end to end along the dimension named above; an argument that names none is the same for every part. Nothing has to cross between parts.
Inputs may be any that keep to these rules, and one draw needn't show every extreme that they name: `clip_id`: never falls along the frames; a clip spans 1 to 8 frames. `frame_decay`: negative.
All inputs are finite; a program needn't handle non-finite values.
Results may differ from a plain program's by a relative error of at most 0.01.
Values may be sent and summed in bfloat16 or wider, within the bound.
No kernel may reach another device: no remote copies, remote signals or barrier semaphores. Data moves between devices by JAX's collectives and lax.ppermute only.
A program may use at most 128 MiB of HBM per device.

v0:
```python
import jax
import jax.numpy as jnp
from jax import lax
from jax.sharding import PartitionSpec as P

HEAD_DIMENSION = 64
WINDOW = 49


EPSILON = 1e-06


def from_behind(value, axis, steps):
    count = lax.axis_size(axis)
    leading, last = (max(0, -steps), min(count, count - steps))
    return lax.ppermute(value, axis, [(source, source + steps) for source in range(leading, last)])


def normalize(values):
    return values * lax.rsqrt(jnp.mean(values * values, axis=-1, keepdims=True) + EPSILON)


def window_attention(queries, keys_all, values_all, window_order):
    frame_count, positions, number_of_heads, head_size = queries.shape
    order_index = window_order[:, :, None, None]

    def arrange(tensor):
        reordered = jnp.take_along_axis(tensor, order_index, axis=1)
        return reordered.reshape(
            frame_count, positions // WINDOW, WINDOW, number_of_heads, head_size
        )

    scores = jnp.einsum(
        "fwihe,fwjhe->fwhij",
        arrange(queries),
        arrange(keys_all),
        preferred_element_type=jnp.float32,
    ) / jnp.sqrt(jnp.float32(head_size))
    weights = jax.nn.softmax(scores, axis=-1).astype(jnp.bfloat16)
    blended = jnp.einsum(
        "fwhij,fwjhe->fwihe", weights, arrange(values_all), preferred_element_type=jnp.float32
    ).astype(jnp.bfloat16)
    blended = blended.reshape(frame_count, positions, number_of_heads, head_size)
    inverse = jnp.argsort(window_order, axis=1)
    return jnp.take_along_axis(blended, inverse[:, :, None, None], axis=1)


def per_device(
    video_tokens,
    window_order,
    clip_id,
    attend_weight,
    attend_out,
    recur_weight,
    frame_decay,
    recur_out,
):
    frame_count, positions, model_width = video_tokens.shape
    local_width = attend_weight.shape[2]
    row_count = frame_count * positions
    inputs = video_tokens.reshape(row_count, model_width).astype(jnp.float32)
    normed = normalize(inputs).astype(jnp.bfloat16)
    projected = jnp.einsum(
        "td,kde->kte", normed, attend_weight, preferred_element_type=jnp.float32
    ).astype(jnp.bfloat16)
    shaped = projected.reshape(
        3, frame_count, positions, local_width // HEAD_DIMENSION, HEAD_DIMENSION
    )
    attended = window_attention(shaped[0], shaped[1], shaped[2], window_order).reshape(
        row_count, local_width
    )
    partial_mix = jnp.dot(attended, attend_out, preferred_element_type=jnp.float32)
    offset = lax.axis_index("head") * local_width
    residual = inputs + lax.psum(partial_mix.astype(jnp.bfloat16), "head").astype(jnp.float32)
    normed_again = normalize(residual).astype(jnp.bfloat16)
    recur_proj = jnp.einsum(
        "td,kde->kte", normed_again, recur_weight, preferred_element_type=jnp.float32
    )
    residual_own = lax.dynamic_slice_in_dim(residual, offset, local_width, 1)
    gate_in = jax.nn.sigmoid(recur_proj[0]).reshape(frame_count, positions, local_width)
    value_in = recur_proj[1].reshape(frame_count, positions, local_width)
    out_gate = jax.nn.silu(recur_proj[2]).reshape(frame_count, positions, local_width)
    retain = jnp.exp(frame_decay)
    driven = jnp.sqrt(1.0 - retain * retain)[:, None, :] * gate_in * value_in
    previous = from_behind(clip_id[frame_count - 1 :], "tm", 1)
    continues = jnp.concatenate(
        [
            (clip_id[:1] == previous).astype(jnp.float32),
            (clip_id[1:] == clip_id[:-1]).astype(jnp.float32),
        ]
    )
    factor = retain * continues[:, None]

    def advance(carried, inputs_now):
        decay_total, state_now = carried
        factor_now, driven_now = inputs_now
        decay_total = factor_now * decay_total
        state_now = factor_now[None, :] * state_now + driven_now
        return ((decay_total, state_now), (decay_total, state_now))

    start_carry = (
        jnp.ones((local_width,), jnp.float32),
        jnp.zeros((positions, local_width), jnp.float32),
    )
    last_carry, all_carry = lax.scan(advance, start_carry, (factor, driven))
    decay_last, state_last = last_carry
    decay_all, state_all = all_carry

    def relay_step(counter, incoming):
        outgoing = decay_last[None, :] * incoming + state_last
        return from_behind(outgoing.astype(jnp.bfloat16), "tm", 1).astype(outgoing.dtype)

    incoming = lax.fori_loop(
        0, lax.axis_size("tm") - 1, relay_step, jnp.zeros((positions, local_width), jnp.float32)
    )
    states = state_all + decay_all[:, None, :] * incoming[None, :, :]
    output_rows = (states * out_gate).astype(jnp.bfloat16).reshape(row_count, local_width)
    partial_out = jnp.dot(output_rows, recur_out, preferred_element_type=jnp.float32)
    result = residual_own + lax.psum_scatter(
        partial_out.astype(jnp.bfloat16), "head", scatter_dimension=1, tiled=True
    ).astype(jnp.float32)
    return result.astype(jnp.bfloat16).reshape(frame_count, positions, local_width)


def solution(mesh):
    return jax.shard_map(
        per_device,
        mesh=mesh,
        in_specs=(
            P(("clip", "tm"), None, None),
            P(("clip", "tm"), None),
            P(("clip", "tm")),
            P(None, None, "head"),
            P("head", None),
            P(None, None, "head"),
            P(("clip", "tm"), "head"),
            P("head", None),
        ),
        out_specs=P(("clip", "tm"), None, "head"),
        check_vma=False,
    )
```

profile of v0, /device:TPU:32, one launch (start us, length us, event | category | flops | bytes accessed | tf_op | source)
XLA Modules:
  0.0 905.4 jit_solution(7665723979493977932)
XLA Ops:
  33.3 28.2 %gather_fusion = bf16[3136,4,64]{2,1,0:T(4,128)(2,1)} fusion(bf16[2,1568,4,64]{3,2,1,0:T(4,128)(2,1)} %reshape.168, s32[3136]{0:T(1024)S(1)} %reshape.147), kind=kCustom, calls=%fused_computation.clone | custom fusion | bytes 3236352 | tf_op jit(solution)/shard_map/jit(take_along_axis)/gather | solution.py:28
  75.9 37.3 %gather_fusion.1 = bf16[3136,4,64]{2,1,0:T(4,128)(2,1)} fusion(bf16[2,1568,4,64]{3,2,1,0:T(4,128)(2,1)} %reshape.170, s32[3136]{0:T(1024)S(1)} %reshape.147), kind=kCustom, calls=%fused_computation.1.clone | custom fusion | bytes 3236352 | tf_op jit(solution)/shard_map/jit(take_along_axis)/gather | solution.py:28
  113.2 9.4 %copy.43 = bf16[2,1568,4,64]{1,0,3,2:T(2,128)(2,1)} copy(bf16[2,1568,4,64]{3,2,1,0:T(4,128)(2,1)} %bitcast.90) | data formatting | bytes 3211264 | tf_op jit(solution)/shard_map/jit(take_along_axis)/gather | solution.py:28
  128.5 28.5 %gather_fusion.2 = bf16[3136,4,64]{2,1,0:T(4,128)(2,1)} fusion(bf16[2,1568,4,64]{3,2,1,0:T(4,128)(2,1)} %reshape.172, s32[3136]{0:T(1024)S(1)} %reshape.147), kind=kCustom, calls=%fused_computation.2.clone | custom fusion | bytes 3236352 | tf_op jit(solution)/shard_map/jit(take_along_axis)/gather | solution.py:28
  157.0 9.3 %copy.47 = bf16[2,1568,4,64]{1,0,3,2:T(2,128)(2,1)} copy(bf16[2,1568,4,64]{3,2,1,0:T(4,128)(2,1)} %bitcast.87) | data formatting | bytes 3211264 | tf_op jit(solution)/shard_map/jit(take_along_axis)/gather | solution.py:28
  173.3 15.7 %reshape.171 = bf16[2,32,49,4,64]{2,1,0,4,3:T(8,128)(2,1)} reshape(bf16[2,1568,4,64]{1,0,3,2:T(2,128)(2,1)} %get-tuple-element.145) | data formatting | bytes 3211264 | tf_op jit(solution)/shard_map/reshape | solution.py:29
  189.0 14.4 %reshape.173 = bf16[2,32,49,4,64]{2,1,0,4,3:T(8,128)(2,1)} reshape(bf16[2,1568,4,64]{1,0,3,2:T(2,128)(2,1)S(1)} %copy-done.3) | data formatting | bytes 3211264 | tf_op jit(solution)/shard_map/reshape | solution.py:29
  203.3 15.2 %fusion.15 = f32[2,32,4,49,49]{3,4,2,1,0:T(8,128)S(1)} fusion(bf16[2,32,49,4,64]{2,1,0,4,3:T(8,128)(2,1)} %reshape.173, bf16[2,32,49,4,64]{2,1,0,4,3:T(8,128)(2,1)} %reshape.171), kind=kOutput, calls=%fused_computation.32 | convolution fusion | flops 78675968 | bytes 5669888 | tf_op jit(solution)/shard_map/fwihe,fwjhe->fwhij/dot_general | solution.py:33
  224.1 14.4 %reshape.169 = bf16[2,32,49,4,64]{2,1,0,4,3:T(8,128)(2,1)} reshape(bf16[2,1568,4,64]{1,0,3,2:T(2,128)(2,1)S(1)} %copy-done.2) | data formatting | bytes 3211264 | tf_op jit(solution)/shard_map/reshape | solution.py:29
  238.5 13.6 %convert_bitcast_fusion = bf16[2,32,49,4,64]{4,2,3,1,0:T(8,128)(2,1)S(1)} fusion(f32[2,32,4,49,49]{3,4,2,1,0:T(8,128)} %get-tuple-element.152, f32[2,32,4,49]{3,2,1,0:T(4,128)S(1)} %get-tuple-element.151, bf16[2,32,49,4,64]{2,1,0,4,3:T(8,128)(2,1)} %reshape.169), kind=kOutput, calls=%fused_computation.37 | convolution fusion | flops 80708096 | bytes 5720064 | tf_op jit(solution)/shard_map/fwhij,fwjhe->fwihe/dot_general | solution.py:40
  255.1 28.3 %gather_fusion.3 = bf16[3136,4,64]{2,1,0:T(4,128)(2,1)} fusion(bf16[2,1568,4,64]{3,2,1,0:T(4,128)(2,1)} %bitcast.91, s32[3136]{0:T(1024)S(1)} %reshape.162), kind=kCustom, calls=%fused_computation.3.clone | custom fusion | bytes 3236352 | tf_op jit(solution)/shard_map/jit(take_along_axis)/gather | solution.py:45
  283.4 8.5 copy.36
  313.3 120.7 %all-reduce.2.cloned.1.call-done = bf16[3136,1024]{1,0:T(8,128)(2,1)} async-done(((bf16[3136,1024]{1,0:T(8,128)(2,1)}), bf16[3136,1024]{1,0:T(8,128)(2,1)}) %all-reduce.2.cloned.1.call-update) | async-done | bytes 6422544 | tf_op jit(solution)/shard_map/psum | solution.py:74
  434.1 12.4 %bitcast_add_fusion.1 = f32[3136,1024]{1,0:T(8,128)} fusion(bf16[2,1568,1024]{2,1,0:T(8,128)(2,1)} %param.14, bf16[3136,1024]{1,0:T(8,128)(2,1)} %all-reduce.2.cloned.1.call-done), kind=kLoop, calls=%fused_computation.13 | loop fusion | flops 9633792 | bytes 25690112 | tf_op jit(solution)/shard_map/add | solution.py:74
  452.2 11.2 %convolution_bitcast_fusion = f32[3,3136,256]{2,1,0:T(8,128)} fusion(bf16[3,1024,256]{2,1,0:T(8,128)(2,1)S(1)} %copy-done.8, f32[3136,1024]{1,0:T(8,128)} %bitcast_add_fusion.1, f32[3136]{0:T(1024)S(1)} %add_rsqrt_fusion), kind=kOutput, calls=%fused_computation.20 | convolution fusion | flops 4938924032 | bytes 24064256 | tf_op jit(solution)/shard_map/td,kde->kte/dot_general | solution.py:76
  478.3 344.1 %while.29 = (s32[]{:T(128)}, f32[1568,256]{1,0:T(8,128)}, f32[256]{0:T(256)S(1)}, f32[1568,256]{1,0:T(8,128)S(1)}, s32[]{:T(128)}, /*index=5*/s32[]{:T(128)}) while((s32[]{:T(128)}, f32[1568,256]{1,0:T(8,128)}, f32[256]{0:T(256)S(1)}, f32[1568,256]{1,0:T(8,128)S(1)}, s32[]{:T(128)}, /*index=5*/s32[]{:T(128)}) %tuple.55), condition=%wide.region_9.11_spmd.clone, body=%wide.region_8.10_spmd.clone.sunk | while | flops 2007043 | bytes 9634935 | solution.py:113
  481.9 20.3 %collective-permute-done = bf16[1568,256]{1,0:T(8,128)(2,1)} collective-permute-done((bf16[1568,256]{1,0:T(8,128)(2,1)S(1)}, bf16[1568,256]{1,0:T(8,128)(2,1)}, u32[]{:S(2)}, u32[]{:S(2)}) %collective-permute-start) | collective-permute-done | bytes 802848 | tf_op jit(solution)/shard_map/while/body/eval_jaxpr/ppermute | solution.py:16
  508.2 20.9 %collective-permute-done = bf16[1568,256]{1,0:T(8,128)(2,1)} collective-permute-done((bf16[1568,256]{1,0:T(8,128)(2,1)S(1)}, bf16[1568,256]{1,0:T(8,128)(2,1)}, u32[]{:S(2)}, u32[]{:S(2)}) %collective-permute-start) | collective-permute-done | bytes 802848 | tf_op jit(solution)/shard_map/while/body/eval_jaxpr/ppermute | solution.py:16
  535.1 20.0 %collective-permute-done = bf16[1568,256]{1,0:T(8,128)(2,1)} collective-permute-done((bf16[1568,256]{1,0:T(8,128)(2,1)S(1)}, bf16[1568,256]{1,0:T(8,128)(2,1)}, u32[]{:S(2)}, u32[]{:S(2)}) %collective-permute-start) | collective-permute-done | bytes 802848 | tf_op jit(solution)/shard_map/while/body/eval_jaxpr/ppermute | solution.py:16
  561.1 19.0 %collective-permute-done = bf16[1568,256]{1,0:T(8,128)(2,1)} collective-permute-done((bf16[1568,256]{1,0:T(8,128)(2,1)S(1)}, bf16[1568,256]{1,0:T(8,128)(2,1)}, u32[]{:S(2)}, u32[]{:S(2)}) %collective-permute-start) | collective-permute-done | bytes 802848 | tf_op jit(solution)/shard_map/while/body/eval_jaxpr/ppermute | solution.py:16
  586.1 18.1 %collective-permute-done = bf16[1568,256]{1,0:T(8,128)(2,1)} collective-permute-done((bf16[1568,256]{1,0:T(8,128)(2,1)S(1)}, bf16[1568,256]{1,0:T(8,128)(2,1)}, u32[]{:S(2)}, u32[]{:S(2)}) %collective-permute-start) | collective-permute-done | bytes 802848 | tf_op jit(solution)/shard_map/while/body/eval_jaxpr/ppermute | solution.py:16
  610.2 17.2 %collective-permute-done = bf16[1568,256]{1,0:T(8,128)(2,1)} collective-permute-done((bf16[1568,256]{1,0:T(8,128)(2,1)S(1)}, bf16[1568,256]{1,0:T(8,128)(2,1)}, u32[]{:S(2)}, u32[]{:S(2)}) %collective-permute-start) | collective-permute-done | bytes 802848 | tf_op jit(solution)/shard_map/while/body/eval_jaxpr/ppermute | solution.py:16
  633.4 16.3 %collective-permute-done = bf16[1568,256]{1,0:T(8,128)(2,1)} collective-permute-done((bf16[1568,256]{1,0:T(8,128)(2,1)S(1)}, bf16[1568,256]{1,0:T(8,128)(2,1)}, u32[]{:S(2)}, u32[]{:S(2)}) %collective-permute-start) | collective-permute-done | bytes 802848 | tf_op jit(solution)/shard_map/while/body/eval_jaxpr/ppermute | solution.py:16
  655.7 15.4 %collective-permute-done = bf16[1568,256]{1,0:T(8,128)(2,1)} collective-permute-done((bf16[1568,256]{1,0:T(8,128)(2,1)S(1)}, bf16[1568,256]{1,0:T(8,128)(2,1)}, u32[]{:S(2)}, u32[]{:S(2)}) %collective-permute-start) | collective-permute-done | bytes 802848 | tf_op jit(solution)/shard_map/while/body/eval_jaxpr/ppermute | solution.py:16
  677.1 14.4 %collective-permute-done = bf16[1568,256]{1,0:T(8,128)(2,1)} collective-permute-done((bf16[1568,256]{1,0:T(8,128)(2,1)S(1)}, bf16[1568,256]{1,0:T(8,128)(2,1)}, u32[]{:S(2)}, u32[]{:S(2)}) %collective-permute-start) | collective-permute-done | bytes 802848 | tf_op jit(solution)/shard_map/while/body/eval_jaxpr/ppermute | solution.py:16
  697.5 14.3 %collective-permute-done = bf16[1568,256]{1,0:T(8,128)(2,1)} collective-permute-done((bf16[1568,256]{1,0:T(8,128)(2,1)S(1)}, bf16[1568,256]{1,0:T(8,128)(2,1)}, u32[]{:S(2)}, u32[]{:S(2)}) %collective-permute-start) | collective-permute-done | bytes 802848 | tf_op jit(solution)/shard_map/while/body/eval_jaxpr/ppermute | solution.py:16
  717.8 14.3 %collective-permute-done = bf16[1568,256]{1,0:T(8,128)(2,1)} collective-permute-done((bf16[1568,256]{1,0:T(8,128)(2,1)S(1)}, bf16[1568,256]{1,0:T(8,128)(2,1)}, u32[]{:S(2)}, u32[]{:S(2)}) %collective-permute-start) | collective-permute-done | bytes 802848 | tf_op jit(solution)/shard_map/while/body/eval_jaxpr/ppermute | solution.py:16
  738.2 15.4 %collective-permute-done = bf16[1568,256]{1,0:T(8,128)(2,1)} collective-permute-done((bf16[1568,256]{1,0:T(8,128)(2,1)S(1)}, bf16[1568,256]{1,0:T(8,128)(2,1)}, u32[]{:S(2)}, u32[]{:S(2)}) %collective-permute-start) | collective-permute-done | bytes 802848 | tf_op jit(solution)/shard_map/while/body/eval_jaxpr/ppermute | solution.py:16
  759.6 16.5 %collective-permute-done = bf16[1568,256]{1,0:T(8,128)(2,1)} collective-permute-done((bf16[1568,256]{1,0:T(8,128)(2,1)S(1)}, bf16[1568,256]{1,0:T(8,128)(2,1)}, u32[]{:S(2)}, u32[]{:S(2)}) %collective-permute-start) | collective-permute-done | bytes 802848 | tf_op jit(solution)/shard_map/while/body/eval_jaxpr/ppermute | solution.py:16
  782.1 17.6 %collective-permute-done = bf16[1568,256]{1,0:T(8,128)(2,1)} collective-permute-done((bf16[1568,256]{1,0:T(8,128)(2,1)S(1)}, bf16[1568,256]{1,0:T(8,128)(2,1)}, u32[]{:S(2)}, u32[]{:S(2)}) %collective-permute-start) | collective-permute-done | bytes 802848 | tf_op jit(solution)/shard_map/while/body/eval_jaxpr/ppermute | solution.py:16
  805.7 14.3 %collective-permute-done = bf16[1568,256]{1,0:T(8,128)(2,1)} collective-permute-done((bf16[1568,256]{1,0:T(8,128)(2,1)S(1)}, bf16[1568,256]{1,0:T(8,128)(2,1)}, u32[]{:S(2)}, u32[]{:S(2)}) %collective-permute-start) | collective-permute-done | bytes 802848 | tf_op jit(solution)/shard_map/while/body/eval_jaxpr/ppermute | solution.py:16
  831.2 63.0 %reduce-scatter.2.cloned.1.call-done = bf16[3136,256]{1,0:T(8,128)(2,1)} async-done(((bf16[3136,1024]{1,0:T(8,128)(2,1)}), bf16[3136,256]{1,0:T(8,128)(2,1)}) %reduce-scatter.2.cloned.1.call-update) | async-done | bytes 1605648 | tf_op jit(solution)/shard_map/reduce_scatter | solution.py:119
  (117 shorter events, 211.0 us)
Async XLA Ops:
  6.5 16.3 %copy-start = (bf16[3,1024,256]{2,1,0:T(8,128)(2,1)S(1)}, bf16[3,1024,256]{2,1,0:T(8,128)(2,1)}, u32[]{:S(2)}) copy-start(bf16[3,1024,256]{2,1,0:T(8,128)(2,1)} %param.17) | copy-start | bytes 4718596
  6.5 427.5 %all-reduce.2.cloned.1.call-start = ((), (), s32[]{:S(2)}) async-start(), calls=%async_computation.1 | async-start | bytes 12845056 | tf_op jit(solution)/shard_map/psum | solution.py:74
  173.3 15.7 %copy-start.3 = (bf16[2,1568,4,64]{1,0,3,2:T(2,128)(2,1)S(1)}, bf16[2,1568,4,64]{1,0,3,2:T(2,128)(2,1)}, u32[]{:S(2)}) copy-start(bf16[2,1568,4,64]{1,0,3,2:T(2,128)(2,1)} %get-tuple-element.146) | copy-start | bytes 4816900
  218.6 5.5 copy-start.2
  291.9 6.4 copy-start.4
  302.8 0.7 copy-start.7
  302.8 10.4 %copy-start.6 = (f32[2,256]{1,0:T(2,128)S(1)}, f32[2,256]{1,0:T(2,128)}, u32[]{:S(2)}) copy-start(f32[2,256]{1,0:T(2,128)} %param.20) | copy-start | bytes 6148
  302.9 591.3 %reduce-scatter.2.cloned.1.call-start = ((), (), s32[]{:S(2)}) async-start(), calls=%async_computation.2 | async-start | bytes 8028160 | tf_op jit(solution)/shard_map/reduce_scatter | solution.py:119
  304.1 7.8 collective-permute-start.1
  446.5 5.7 copy-start.8
  478.5 23.7 %collective-permute-start = (bf16[1568,256]{1,0:T(8,128)(2,1)S(1)}, bf16[1568,256]{1,0:T(8,128)(2,1)}, u32[]{:S(2)}, u32[]{:S(2)}) collective-permute-start(bf16[1568,256]{1,0:T(8,128)(2,1)S(1)} %fusion.38), channel_id=1, source_target_pairs={{0,4},{4,8},{8,12},{12,16},{16,20},{20,24},{24,28},{28,32},{32,36}... | collective-permute-start | bytes 2408456 | tf_op jit(solution)/shard_map/while/body/eval_jaxpr/ppermute | solution.py:16
  506.3 22.8 %collective-permute-start = (bf16[1568,256]{1,0:T(8,128)(2,1)S(1)}, bf16[1568,256]{1,0:T(8,128)(2,1)}, u32[]{:S(2)}, u32[]{:S(2)}) collective-permute-start(bf16[1568,256]{1,0:T(8,128)(2,1)S(1)} %fusion.38), channel_id=1, source_target_pairs={{0,4},{4,8},{8,12},{12,16},{16,20},{20,24},{24,28},{28,32},{32,36}... | collective-permute-start | bytes 2408456 | tf_op jit(solution)/shard_map/while/body/eval_jaxpr/ppermute | solution.py:16
  533.2 21.9 %collective-permute-start = (bf16[1568,256]{1,0:T(8,128)(2,1)S(1)}, bf16[1568,256]{1,0:T(8,128)(2,1)}, u32[]{:S(2)}, u32[]{:S(2)}) collective-permute-start(bf16[1568,256]{1,0:T(8,128)(2,1)S(1)} %fusion.38), channel_id=1, source_target_pairs={{0,4},{4,8},{8,12},{12,16},{16,20},{20,24},{24,28},{28,32},{32,36}... | collective-permute-start | bytes 2408456 | tf_op jit(solution)/shard_map/while/body/eval_jaxpr/ppermute | solution.py:16
  559.2 21.0 %collective-permute-start = (bf16[1568,256]{1,0:T(8,128)(2,1)S(1)}, bf16[1568,256]{1,0:T(8,128)(2,1)}, u32[]{:S(2)}, u32[]{:S(2)}) collective-permute-start(bf16[1568,256]{1,0:T(8,128)(2,1)S(1)} %fusion.38), channel_id=1, source_target_pairs={{0,4},{4,8},{8,12},{12,16},{16,20},{20,24},{24,28},{28,32},{32,36}... | collective-permute-start | bytes 2408456 | tf_op jit(solution)/shard_map/while/body/eval_jaxpr/ppermute | solution.py:16
  584.2 20.1 %collective-permute-start = (bf16[1568,256]{1,0:T(8,128)(2,1)S(1)}, bf16[1568,256]{1,0:T(8,128)(2,1)}, u32[]{:S(2)}, u32[]{:S(2)}) collective-permute-start(bf16[1568,256]{1,0:T(8,128)(2,1)S(1)} %fusion.38), channel_id=1, source_target_pairs={{0,4},{4,8},{8,12},{12,16},{16,20},{20,24},{24,28},{28,32},{32,36}... | collective-permute-start | bytes 2408456 | tf_op jit(solution)/shard_map/while/body/eval_jaxpr/ppermute | solution.py:16
  608.3 19.1 %collective-permute-start = (bf16[1568,256]{1,0:T(8,128)(2,1)S(1)}, bf16[1568,256]{1,0:T(8,128)(2,1)}, u32[]{:S(2)}, u32[]{:S(2)}) collective-permute-start(bf16[1568,256]{1,0:T(8,128)(2,1)S(1)} %fusion.38), channel_id=1, source_target_pairs={{0,4},{4,8},{8,12},{12,16},{16,20},{20,24},{24,28},{28,32},{32,36}... | collective-permute-start | bytes 2408456 | tf_op jit(solution)/shard_map/while/body/eval_jaxpr/ppermute | solution.py:16
  631.5 18.2 %collective-permute-start = (bf16[1568,256]{1,0:T(8,128)(2,1)S(1)}, bf16[1568,256]{1,0:T(8,128)(2,1)}, u32[]{:S(2)}, u32[]{:S(2)}) collective-permute-start(bf16[1568,256]{1,0:T(8,128)(2,1)S(1)} %fusion.38), channel_id=1, source_target_pairs={{0,4},{4,8},{8,12},{12,16},{16,20},{20,24},{24,28},{28,32},{32,36}... | collective-permute-start | bytes 2408456 | tf_op jit(solution)/shard_map/while/body/eval_jaxpr/ppermute | solution.py:16
  653.8 17.3 %collective-permute-start = (bf16[1568,256]{1,0:T(8,128)(2,1)S(1)}, bf16[1568,256]{1,0:T(8,128)(2,1)}, u32[]{:S(2)}, u32[]{:S(2)}) collective-permute-start(bf16[1568,256]{1,0:T(8,128)(2,1)S(1)} %fusion.38), channel_id=1, source_target_pairs={{0,4},{4,8},{8,12},{12,16},{16,20},{20,24},{24,28},{28,32},{32,36}... | collective-permute-start | bytes 2408456 | tf_op jit(solution)/shard_map/while/body/eval_jaxpr/ppermute | solution.py:16
  675.1 16.4 %collective-permute-start = (bf16[1568,256]{1,0:T(8,128)(2,1)S(1)}, bf16[1568,256]{1,0:T(8,128)(2,1)}, u32[]{:S(2)}, u32[]{:S(2)}) collective-permute-start(bf16[1568,256]{1,0:T(8,128)(2,1)S(1)} %fusion.38), channel_id=1, source_target_pairs={{0,4},{4,8},{8,12},{12,16},{16,20},{20,24},{24,28},{28,32},{32,36}... | collective-permute-start | bytes 2408456 | tf_op jit(solution)/shard_map/while/body/eval_jaxpr/ppermute | solution.py:16
  695.6 16.3 %collective-permute-start = (bf16[1568,256]{1,0:T(8,128)(2,1)S(1)}, bf16[1568,256]{1,0:T(8,128)(2,1)}, u32[]{:S(2)}, u32[]{:S(2)}) collective-permute-start(bf16[1568,256]{1,0:T(8,128)(2,1)S(1)} %fusion.38), channel_id=1, source_target_pairs={{0,4},{4,8},{8,12},{12,16},{16,20},{20,24},{24,28},{28,32},{32,36}... | collective-permute-start | bytes 2408456 | tf_op jit(solution)/shard_map/while/body/eval_jaxpr/ppermute | solution.py:16
  715.9 16.3 %collective-permute-start = (bf16[1568,256]{1,0:T(8,128)(2,1)S(1)}, bf16[1568,256]{1,0:T(8,128)(2,1)}, u32[]{:S(2)}, u32[]{:S(2)}) collective-permute-start(bf16[1568,256]{1,0:T(8,128)(2,1)S(1)} %fusion.38), channel_id=1, source_target_pairs={{0,4},{4,8},{8,12},{12,16},{16,20},{20,24},{24,28},{28,32},{32,36}... | collective-permute-start | bytes 2408456 | tf_op jit(solution)/shard_map/while/body/eval_jaxpr/ppermute | solution.py:16
  736.3 17.3 %collective-permute-start = (bf16[1568,256]{1,0:T(8,128)(2,1)S(1)}, bf16[1568,256]{1,0:T(8,128)(2,1)}, u32[]{:S(2)}, u32[]{:S(2)}) collective-permute-start(bf16[1568,256]{1,0:T(8,128)(2,1)S(1)} %fusion.38), channel_id=1, source_target_pairs={{0,4},{4,8},{8,12},{12,16},{16,20},{20,24},{24,28},{28,32},{32,36}... | collective-permute-start | bytes 2408456 | tf_op jit(solution)/shard_map/while/body/eval_jaxpr/ppermute | solution.py:16
  757.7 18.4 %collective-permute-start = (bf16[1568,256]{1,0:T(8,128)(2,1)S(1)}, bf16[1568,256]{1,0:T(8,128)(2,1)}, u32[]{:S(2)}, u32[]{:S(2)}) collective-permute-start(bf16[1568,256]{1,0:T(8,128)(2,1)S(1)} %fusion.38), channel_id=1, source_target_pairs={{0,4},{4,8},{8,12},{12,16},{16,20},{20,24},{24,28},{28,32},{32,36}... | collective-permute-start | bytes 2408456 | tf_op jit(solution)/shard_map/while/body/eval_jaxpr/ppermute | solution.py:16
  780.2 19.5 %collective-permute-start = (bf16[1568,256]{1,0:T(8,128)(2,1)S(1)}, bf16[1568,256]{1,0:T(8,128)(2,1)}, u32[]{:S(2)}, u32[]{:S(2)}) collective-permute-start(bf16[1568,256]{1,0:T(8,128)(2,1)S(1)} %fusion.38), channel_id=1, source_target_pairs={{0,4},{4,8},{8,12},{12,16},{16,20},{20,24},{24,28},{28,32},{32,36}... | collective-permute-start | bytes 2408456 | tf_op jit(solution)/shard_map/while/body/eval_jaxpr/ppermute | solution.py:16
  803.7 16.3 %collective-permute-start = (bf16[1568,256]{1,0:T(8,128)(2,1)S(1)}, bf16[1568,256]{1,0:T(8,128)(2,1)}, u32[]{:S(2)}, u32[]{:S(2)}) collective-permute-start(bf16[1568,256]{1,0:T(8,128)(2,1)S(1)} %fusion.38), channel_id=1, source_target_pairs={{0,4},{4,8},{8,12},{12,16},{16,20},{20,24},{24,28},{28,32},{32,36}... | collective-permute-start | bytes 2408456 | tf_op jit(solution)/shard_map/while/body/eval_jaxpr/ppermute | solution.py:16
  822.4 4.3 copy-start.5
  831.2 66.9 %copy-start.1 = (bf16[3,1024,256]{2,1,0:T(8,128)(2,1)S(1)}, bf16[3,1024,256]{2,1,0:T(8,128)(2,1)}, u32[]{:S(2)}) copy-start(bf16[3,1024,256]{2,1,0:T(8,128)(2,1)} %param.17) | copy-start | bytes 4718596
Sparse Core Ops, SparseCore 0:
  303.0 131.0 all-reduce.1
  831.3 62.8 reduce-scatter.1
where the time goes:
time: 916 us; the launch traced here: 905 us
  waiting for transfers between devices  441 us (48%)
  local copies, waits for them, and re-layouts  227 us (25%)
  other arithmetic  132 us (14%)
  matrix products  54.5 us (6%)
  starting transfers between devices  33.7 us (4%)
  between operations  16.6 us (2%)
    ppermute x16, waiting for transfers between devices, from_behind(): lax.ppermute(value, axis, [(source, source + steps) for source in range(l...  257 us
    gather x7, local copies, waits for them, and re-layouts, arrange(): reordered = jnp.take_along_axis(tensor, order_index, axis=1)  121 us
    psum x1, waiting for transfers between devices, per_device(): lax.psum(partial_mix.astype(jnp.bfloat16), 'head').astype(jnp.float32)  121 us
    reduce_scatter x1, waiting for transfers between devices, per_device(): lax.psum_scatter(partial_out.astype(jnp.bfloat16), 'head', scatter_dimens...  63 us
    reshape x3, local copies, waits for them, and re-layouts, arrange(): reordered.reshape(frame_count, positions // WINDOW, WINDOW, number_of_hea...  44.4 us
    gather x3, local copies, waits for them, and re-layouts, window_attention(): return jnp.take_along_axis(blended, inverse[:, :, None, None], axis=1)  36.8 us
    convert_element_type x15, other arithmetic, relay_step(): from_behind(outgoing.astype(jnp.bfloat16), 'tm', 1).astype(outgoing.dtype)  36.2 us
    ppermute x16, starting transfers between devices, from_behind(): lax.ppermute(value, axis, [(source, source + steps) for source in range(l...  33.7 us
  transfers between devices with their start and end apart: 18, of which 18 were waited for; matrix products, arithmetic and copies ran while one was open for 0% of the time, Pallas kernels for 0%

commit v1 on v0

v1 whole, which is shorter than its diff:
```python
import functools
import jax
import jax.numpy as jnp
from jax import lax
from jax.experimental import pallas as pl
from jax.experimental.pallas import tpu as pltpu
from jax.sharding import Mesh, PartitionSpec as P

HEAD = 64
WINDOW = 49
SLOT = 64
TOK = 1568
WINDOWS = TOK // WINDOW
ROWS = WINDOWS * SLOT
D = 1024
C = 256
FRAMES = 2
QUARTER = TOK // 4
STRIDE = 96
SHARE = 104
SENT = SHARE + 8
EPSILON = 1e-06
F32 = jnp.float32
BF16 = jnp.bfloat16
LIMIT = 60 * 1024 * 1024


def dot(left, right):
    return jnp.dot(left, right, preferred_element_type=F32)


def dot_t(left, right):
    return lax.dot_general(left, right, (((1,), (1,)), ((), ())), preferred_element_type=F32)


def scaled(values):
    return values * lax.rsqrt(jnp.mean(values * values, axis=-1, keepdims=True) + EPSILON)


def attend_kernel(x_ref, column_ref, row_ref, decay_ref, continues_ref, weight_ref, out_ref, normed, qkv, arranged, mixed):
    step = 112

    def norm_step(i, carry):
        rows = pl.ds(pl.multiple_of(i * step, 16), step)
        normed[rows, :] = scaled(x_ref[0, rows, :].astype(F32)).astype(BF16)
        return carry

    lax.fori_loop(0, TOK // step, norm_step, 0)

    half = TOK // 2
    for i in range(2):
        for k in range(3):
            rows = slice(i * half, (i + 1) * half)
            qkv[rows, k * C : (k + 1) * C] = dot(normed[rows, :], weight_ref[k]).astype(BF16)

    part = 512

    def arrange_step(i, carry):
        rows = pl.ds(pl.multiple_of(i * part, part), part)
        lanes = lax.broadcasted_iota(jnp.int32, (part, TOK), 1)
        pick = jnp.where(lanes == column_ref[0, rows, :], 1.0, 0.0).astype(BF16)
        arranged[rows, :] = dot(pick, qkv[...]).astype(BF16)
        return carry

    lax.fori_loop(0, ROWS // part, arrange_step, 0)

    lane_head = lax.broadcasted_iota(jnp.int32, (SLOT, C), 1) // HEAD
    own = [lane_head == h for h in range(4)]
    row_index = lax.broadcasted_iota(jnp.int32, (C, C), 0)
    lane_index = lax.broadcasted_iota(jnp.int32, (C, C), 1)
    together = jnp.where(row_index // HEAD == lane_index // HEAD, 1.0, 0.0).astype(BF16)
    group = 4
    lane = lax.broadcasted_iota(jnp.int32, (group * SLOT, 128), 1)
    low = lane < SLOT
    valid = (lane % SLOT) < WINDOW
    floor = -3.0e38

    def spread(block):
        return jnp.concatenate([jnp.where(own[h], block, jnp.zeros_like(block)) for h in range(4)], axis=0)

    def window_step(i, carry):
        base = i * (group * SLOT)
        scores = []
        for w in range(group):
            rows = pl.ds(pl.multiple_of(base + w * SLOT, SLOT), SLOT)
            scores.append(dot_t(arranged[rows, 0:C], spread(arranged[rows, C : 2 * C])))
        scores = jnp.concatenate(scores, axis=0) * 0.125
        pieces = []
        for side in range(2):
            piece = jnp.where(valid, scores[:, side * 128 : (side + 1) * 128], floor)
            top_low = jnp.max(jnp.where(low, piece, floor), axis=-1, keepdims=True)
            top_high = jnp.max(jnp.where(low, floor, piece), axis=-1, keepdims=True)
            pieces.append(jnp.exp(piece - jnp.where(low, top_low, top_high)))
        weights = jnp.concatenate(pieces, axis=1).astype(BF16)
        totals = dot(weights, together)
        blended = []
        for w in range(group):
            rows = pl.ds(pl.multiple_of(base + w * SLOT, SLOT), SLOT)
            blended.append(dot(weights[w * SLOT : (w + 1) * SLOT], spread(arranged[rows, 2 * C : 3 * C])))
        blended = jnp.concatenate(blended, axis=0) / totals
        mixed[pl.ds(pl.multiple_of(base, group * SLOT), group * SLOT), :] = blended.astype(BF16)
        return carry

    lax.fori_loop(0, WINDOWS // group, window_step, 0)

    decay = decay_ref[0]
    high = decay.astype(BF16).astype(F32)
    middle = (decay - high).astype(BF16).astype(F32)
    index = lax.broadcasted_iota(jnp.int32, (8, C), 0)
    extra = jnp.where(
        index == 0,
        high,
        jnp.where(index == 1, middle, jnp.where(index == 2, (decay - high) - middle, continues_ref[0])),
    ).astype(BF16)

    def restore_step(i, carry):
        r = lax.broadcasted_iota(jnp.int32, (4 * SHARE, ROWS), 0)
        late = jnp.where(r >= SHARE, 8, 0) + jnp.where(r >= 2 * SHARE, 8, 0) + jnp.where(r >= 3 * SHARE, 8, 0)
        position = r - late + i * QUARTER
        pick = jnp.where(position == row_ref[0], 1.0, 0.0).astype(BF16)
        result = dot(pick, mixed[...])
        for h in range(4):
            out_ref[4 * i + h, 0, :SHARE, :] = result[h * SHARE : (h + 1) * SHARE].astype(BF16)
            out_ref[4 * i + h, 0, SHARE:, :] = extra
        return carry

    lax.fori_loop(0, 4, restore_step, 0)


def attend(tokens, window_order, frame_decay, continues, weight):
    padded = jnp.pad(
        window_order.reshape(FRAMES, WINDOWS, WINDOW),
        ((0, 0), (0, 0), (0, SLOT - WINDOW)),
        constant_values=-1,
    ).reshape(FRAMES, ROWS)
    return pl.pallas_call(
        attend_kernel,
        grid=(FRAMES,),
        in_specs=[
            pl.BlockSpec((1, TOK, D), lambda f: (f, 0, 0)),
            pl.BlockSpec((1, ROWS, 1), lambda f: (f, 0, 0)),
            pl.BlockSpec((1, 1, ROWS), lambda f: (f, 0, 0)),
            pl.BlockSpec((1, 1, C), lambda f: (f, 0, 0)),
            pl.BlockSpec((1, 1, C), lambda f: (f, 0, 0)),
            pl.BlockSpec((3, D, C), lambda f: (0, 0, 0)),
        ],
        out_specs=pl.BlockSpec((16, 1, SENT, C), lambda f: (0, f, 0, 0)),
        out_shape=jax.ShapeDtypeStruct((16, FRAMES, SENT, C), BF16),
        scratch_shapes=[
            pltpu.VMEM((TOK, D), BF16),
            pltpu.VMEM((TOK, 3 * C), BF16),
            pltpu.VMEM((ROWS, 3 * C), BF16),
            pltpu.VMEM((ROWS, C), BF16),
        ],
        compiler_params=pltpu.CompilerParams(vmem_limit_bytes=LIMIT),
        cost_estimate=pl.CostEstimate(
            flops=2 * FRAMES * (TOK * D * 3 * C + ROWS * TOK * 3 * C + 4 * ROWS * C * C + ROWS * TOK * C),
            bytes_accessed=FRAMES * TOK * D * 4,
            transcendentals=FRAMES * ROWS * C,
        ),
        name="attend",
    )(tokens, padded[:, :, None], padded[:, None, :], frame_decay[:, None, :], continues, weight)


def recur_kernel(
    place_ref, att_ref, x0_ref, x1_ref, x2_ref, x3_ref, mix_ref, gate_ref, value_ref, open_ref,
    residual_ref, state_ref, decay_ref, open_out_ref, last_ref,
    normed,
):
    x = place_ref[0]
    h = pl.program_id(0)
    count = FRAMES * SHARE

    @pl.when(h == 0)
    def _():
        for s, x_ref in enumerate((x0_ref, x1_ref, x2_ref, x3_ref)):
            source = lax.rem(x + (4 - s), 4)
            pieces = []
            for c in range(2):
                for q in range(2):
                    total = None
                    for k in range(4):
                        left = att_ref[4 * source + k, :, :SHARE, :].reshape(count, C)
                        term = dot(left, mix_ref[c, k, q * C : (q + 1) * C, :])
                        total = term if total is None else total + term
                    pieces.append(total)
            residual = x_ref[...].reshape(count, D).astype(F32) + jnp.concatenate(pieces, axis=1)
            residual_ref[source] = residual
            normed[source] = scaled(residual).astype(BF16)

    rows = normed[...].reshape(4 * count, D)

    def project(ref):
        return dot(rows[:, : D // 2], ref[0, 0]) + dot(rows[:, D // 2 :], ref[1, 0])

    driven = jax.nn.sigmoid(project(gate_ref)) * project(value_ref)
    opening = project(open_ref)
    open_out_ref[0] = opening * jax.nn.sigmoid(opening)
    state = jnp.zeros((SHARE, C), F32)
    decay = jnp.ones((1, C), F32)
    for f in range(4 * FRAMES):
        extra = att_ref[(f // 2) * 4 + h, f % 2, SHARE:, :].astype(F32)
        retain = jnp.exp(extra[0:1] + extra[1:2] + extra[2:3])
        factor = retain * extra[3:4]
        drive = jnp.sqrt(1.0 - retain * retain)
        decay = factor * decay
        state = factor * state + drive * driven[f * SHARE : (f + 1) * SHARE]
        state_ref[0, f * SHARE : (f + 1) * SHARE, :] = state
        decay_ref[0, f : f + 1, :] = decay
    last_ref[0] = state.astype(BF16)


def finish_kernel(state_ref, decay_ref, open_ref, incoming_ref, residual_ref, weight_ref, out_ref, rows):
    n = pl.program_id(0)

    @pl.when(n == 0)
    def _():
        for k in range(4):
            incoming = incoming_ref[k].astype(F32)
            for f in range(4 * FRAMES):
                piece = slice(f * SHARE, (f + 1) * SHARE)
                state = state_ref[k, piece, :] + decay_ref[k, f : f + 1, :] * incoming
                rows[k, piece, :] = (state * open_ref[k, piece, :]).astype(BF16)

    total = residual_ref[...].reshape(8 * SHARE, C)
    for k in range(4):
        total = total + dot(rows[k], weight_ref[0, k])
    out_ref[...] = total.reshape(4, 1, FRAMES, SHARE, C).astype(BF16)


def place_kernel(in_ref, out_ref):
    for k in range(4):
        size = STRIDE if k < 3 else SHARE
        for f in range(FRAMES):
            out_ref[f, 0, k * STRIDE : k * STRIDE + size, :] = in_ref[0, k, f, :size, :]


def per_device(tokens, window_order, clip_id, attend_weight, attend_out, recur_weight, frame_decay, recur_out):
    c, z, x, h = (lax.axis_index(name) for name in ("clip", "z", "x", "head"))

    def column_blocks(weight):
        blocks = weight.reshape(C, 4, C).transpose(1, 0, 2)
        return lax.dynamic_slice_in_dim(blocks, 2 * c, 2, 0).reshape(2 * C, C)

    half = lax.dynamic_slice_in_dim(recur_weight, c * (D // 2), D // 2, 1).reshape(3 * D // 2, C)
    packed = jnp.concatenate([column_blocks(attend_out), half, column_blocks(recur_out)], axis=0)
    before = lax.ppermute(clip_id[1:], ("z", "x"), [(i, i + 1) for i in range(15)])
    continues = (clip_id == jnp.concatenate([before, clip_id[:1]])).astype(F32)
    continues = continues * jnp.where((jnp.arange(FRAMES) > 0) | (z > 0) | (x > 0), 1.0, 0.0)
    continues = jnp.broadcast_to(continues[:, None, None], (FRAMES, 1, C))
    weights = lax.all_gather(packed, ("clip", "head"), axis=0).reshape(2, 4, 5 * D // 2, C)

    quarters = tokens.reshape(FRAMES, 4, QUARTER, D)
    moved = []
    for s in range(4):
        block = lax.dynamic_slice(
            quarters, (0, lax.rem(x + s, 4), h * STRIDE, 0), (FRAMES, 1, SHARE, D)
        ).reshape(FRAMES, SHARE, D)
        if s:
            block = lax.ppermute(block, "x", [(i, (i + s) % 4) for i in range(4)])
        moved.append(block)

    mixed = attend(tokens, window_order, frame_decay, continues, attend_weight)
    mixed = lax.all_to_all(mixed, ("x", "head"), 0, 0)

    whole = lambda shape: pl.BlockSpec(shape, lambda n: (0,) * len(shape))
    span = D // 2
    wide = 8 * SHARE
    residual, state, decay, opened, last = pl.pallas_call(
        recur_kernel,
        grid=(4,),
        in_specs=[
            pl.BlockSpec(memory_space=pltpu.SMEM),
            whole((16, FRAMES, SENT, C)),
            whole((FRAMES, SHARE, D)),
            whole((FRAMES, SHARE, D)),
            whole((FRAMES, SHARE, D)),
            whole((FRAMES, SHARE, D)),
            pl.BlockSpec((2, 4, span, C), lambda n: (0, 0, 0, 0)),
            pl.BlockSpec((2, 1, span, C), lambda n: (0, n, 1, 0)),
            pl.BlockSpec((2, 1, span, C), lambda n: (0, n, 2, 0)),
            pl.BlockSpec((2, 1, span, C), lambda n: (0, n, 3, 0)),
        ],
        out_specs=[
            whole((4, FRAMES * SHARE, D)),
            pl.BlockSpec((1, wide, C), lambda n: (n, 0, 0)),
            pl.BlockSpec((1, 8, C), lambda n: (n, 0, 0)),
            pl.BlockSpec((1, wide, C), lambda n: (n, 0, 0)),
            pl.BlockSpec((1, SHARE, C), lambda n: (n, 0, 0)),
        ],
        out_shape=[
            jax.ShapeDtypeStruct((4, FRAMES * SHARE, D), F32),
            jax.ShapeDtypeStruct((4, wide, C), F32),
            jax.ShapeDtypeStruct((4, 8, C), F32),
            jax.ShapeDtypeStruct((4, wide, C), F32),
            jax.ShapeDtypeStruct((4, SHARE, C), BF16),
        ],
        scratch_shapes=[pltpu.VMEM((4, FRAMES * SHARE, D), BF16)],
        compiler_params=pltpu.CompilerParams(vmem_limit_bytes=LIMIT),
        name="recur",
    )(x[None], mixed, *moved, weights, weights, weights, weights)

    incoming = lax.ppermute(last, "z", [(i, i + 1) for i in range(3)])

    result = pl.pallas_call(
        finish_kernel,
        grid=(4,),
        in_specs=[
            whole((4, wide, C)),
            whole((4, 8, C)),
            whole((4, wide, C)),
            whole((4, SHARE, C)),
            pl.BlockSpec((4, FRAMES * SHARE, C), lambda n: (0, 0, n)),
            pl.BlockSpec((1, 4, C, C), lambda n: (n // 2, 0, 8 + n % 2, 0)),
        ],
        out_specs=pl.BlockSpec((4, 1, FRAMES, SHARE, C), lambda n: (0, n, 0, 0, 0)),
        out_shape=jax.ShapeDtypeStruct((4, 4, FRAMES, SHARE, C), BF16),
        scratch_shapes=[pltpu.VMEM((4, wide, C), BF16)],
        compiler_params=pltpu.CompilerParams(vmem_limit_bytes=LIMIT),
        name="finish",
    )(state, decay, opened, incoming, residual, weights)

    result = lax.all_to_all(result.reshape(16, FRAMES, SHARE, C), ("x", "head"), 0, 0)
    placed = pl.pallas_call(
        place_kernel,
        grid=(4,),
        in_specs=[pl.BlockSpec((1, 4, FRAMES, SHARE, C), lambda n: (n, 0, 0, 0, 0))],
        out_specs=pl.BlockSpec((FRAMES, 1, QUARTER, C), lambda n: (0, n, 0, 0)),
        out_shape=jax.ShapeDtypeStruct((FRAMES, 4, QUARTER, C), BF16),
        name="place",
    )(result.reshape(4, 4, FRAMES, SHARE, C))
    return placed.reshape(FRAMES, TOK, C)


def solution(mesh):
    split = Mesh(mesh.devices.reshape(2, 4, 4, 4), ("clip", "z", "x", "head"))
    frames = ("clip", "z", "x")
    return jax.shard_map(
        per_device,
        mesh=split,
        in_specs=(
            P(frames, None, None),
            P(frames, None),
            P(frames),
            P(None, None, "head"),
            P("head", None),
            P(None, None, "head"),
            P(frames, "head"),
            P("head", None),
        ),
        out_specs=P(frames, None, "head"),
        check_vma=False,
    )
```

time: 916 us -> 182 us (0.20); the launches traced: 905 us -> 181 us
  waiting for transfers between devices: 441 us -> 37.4 us
  local copies, waits for them, and re-layouts: 227 us -> 14.8 us
  other arithmetic: 132 us -> 2.49 us
  Pallas kernels: 0 us -> 66.6 us
  matrix products: 54.5 us -> 0 us
  blocking collectives: 0 us -> 27.3 us
  starting transfers between devices: 33.7 us -> 19.1 us
    ppermute x16 -> x5, waiting for transfers between devices: 257 us -> 37.4 us  [the longest x3 33 us: per_device(): block = lax.ppermute(block, 'x', [(i, (i + s) % 4) for i in range(4)])]
    gather x10 -> x0, local copies, waits for them, and re-layouts: 158 us -> none  [the longest x7 121 us: arrange(): reordered = jnp.take_along_axis(tensor, order_index, axis=1)]
    psum x1 -> x0, waiting for transfers between devices: 121 us -> none  [per_device(): lax.psum(partial_mix.astype(jnp.bfloat16), 'head').astype(jnp.float32)]
    convert_element_type x33 -> x0, other arithmetic: 71.6 us -> none  [the longest x15 36.2 us: relay_step(): from_behind(outgoing.astype(jnp.bfloat16), 'tm', 1).astype(outgoing.dtype)]
    pallas_call x0 -> x4, Pallas kernels: none -> 66.6 us  [the longest x1 41.1 us: attend(): pl.pallas_call(attend_kernel, grid=(FRAMES,), in_specs=[pl.BlockSpec((1,...]
    reduce_scatter x1 -> x0, waiting for transfers between devices: 63 us -> none  [per_device(): lax.psum_scatter(partial_out.astype(jnp.bfloat16), 'head', scatter_dimens...]
    dot_general x6 -> x0, matrix products: 54.5 us -> none  [the longest x1 15.2 us: window_attention(): jnp.einsum('fwihe,fwjhe->fwhij', arrange(queries), arrange(keys_all), pre...]
    reshape x5 -> x4, local copies, waits for them, and re-layouts: 51 us -> 5.46 us  [the longest x2 2.99 us: column_blocks(): blocks = weight.reshape(C, 4, C).transpose(1, 0, 2)]
  transfers between devices with their start and end apart: 18 -> 7, of which waited for: 18 -> 4; matrix products, arithmetic and copies ran while one was open for 0% -> 5% of each run, Pallas kernels for 0% -> 23%
where the time goes in v1:
time: 182 us; the launch traced here: 181 us
  Pallas kernels  66.6 us (37%)
  waiting for transfers between devices  37.4 us (21%)
  blocking collectives  27.3 us (15%)
  starting transfers between devices  19.1 us (10%)
  local copies, waits for them, and re-layouts  14.8 us (8%)
  between operations  13.6 us (7%)
  other arithmetic  2.49 us (1%)
    pallas_call x1, Pallas kernels, attend(): pl.pallas_call(attend_kernel, grid=(FRAMES,), in_specs=[pl.BlockSpec((1,...  41.1 us
    ppermute x3, waiting for transfers between devices, per_device(): block = lax.ppermute(block, 'x', [(i, (i + s) % 4) for i in range(4)])  33 us
    all_to_all x1, blocking collectives, per_device(): lax.all_to_all(result.reshape(16, FRAMES, SHARE, C), ('x', 'head'), 0, 0)  27.3 us
    pallas_call x1, Pallas kernels, per_device(): pl.pallas_call(recur_kernel, grid=(4,), in_specs=[pl.BlockSpec(memory_spa...  13.8 us
    pallas_call x1, Pallas kernels, per_device(): pl.pallas_call(finish_kernel, grid=(4,), in_specs=[whole((4, wide, C)), w...  8.09 us
    all_to_all x1, starting transfers between devices, per_device(): mixed = lax.all_to_all(mixed, ('x', 'head'), 0, 0)  7.4 us
    ppermute x3, starting transfers between devices, per_device(): block = lax.ppermute(block, 'x', [(i, (i + s) % 4) for i in range(4)])  4.8 us
    ppermute x1, waiting for transfers between devices, per_device(): incoming = lax.ppermute(last, 'z', [(i, i + 1) for i in range(3)])  4.4 us
  transfers between devices with their start and end apart: 7, of which 4 were waited for; matrix products, arithmetic and copies ran while one was open for 5% of the time, Pallas kernels for 23%

profile of v1, /device:TPU:32, one launch (start us, length us, event | category | flops | bytes accessed | tf_op | source)
XLA Modules:
  0.0 181.3 jit_solution(4573735619678758686)
XLA Ops:
  6.5 1.6 reshape.54
  8.1 1.4 reshape.57
  9.5 0.5 dynamic-slice_bitcast_fusion.4
  10.2 0.1 constant_dynamic-slice_fusion
  10.3 1.1 pad_maximum_fusion
  11.4 0.0 all-gather.3.cloned.1.call-update
  11.5 0.6 fusion
  12.0 3.4 %collective-permute-start = (s32[1]{0:T(128)}, s32[1]{0:T(128)}, u32[]{:S(2)}, u32[]{:S(2)}) collective-permute-start(s32[1]{0:T(128)} %get-tuple-element.19), channel_id=1, source_target_pairs={{0,4},{4,8},{8,12},{12,16},{16,20},{20,24},{24,28},{28,32},{32,36}... | collective-permute-start | bytes 20 | tf_op jit(solution)/shard_map/ppermute | solution.py:247
  15.5 0.1 reshape.48
  15.6 0.7 broadcast_in_dim_reshape.7.row_ref
  16.3 3.4 %broadcast_in_dim_reshape.8.column_ref = s32[2,2048,1]{2,1,0:T(8,128)} reshape(s32[2,32,64]{2,1,0:T(8,128)S(1)} %pad.4) | data formatting | bytes 32768 | tf_op jit(solution)/shard_map/broadcast_in_dim;reshape | solution.py:162
  19.7 0.6 broadcast_in_dim.21.decay_ref
  20.3 1.3 compare_select_fusion
  21.6 0.7 broadcast_in_dim.24.continues_ref
  22.3 41.1 %attend.1 = bf16[16,2,112,256]{3,2,1,0:T(8,128)(2,1)} custom-call(bf16[2,1568,1024]{2,1,0:T(8,128)(2,1)} %x_ref.1, s32[2,2048,1]{2,1,0:T(8,128)} %broadcast_in_dim_reshape.8.column_ref, s32[2,1,2048]{2,1,0:T(1,128)} %broadcast_in_dim_reshape.7.row_ref, f32[2,1,256]{2,1,0:T(1,128)} %broadcast_in_dim.21.decay_ref, ...), custom_call_target="tpu_custom_call" | custom-call | flops 20233322496 | bytes 12845056 | tf_op jit(solution)/shard_map/attend/pallas_call | solution.py:136
  63.4 7.4 %all-to-all-start = ((bf16[16,2,112,256]{3,2,1,0:T(8,128)(2,1)}), bf16[16,2,112,256]{3,2,1,0:T(8,128)(2,1)S(1)}, u32[]{:S(2)}, u32[]{:S(2)}) async-start(bf16[16,2,112,256]{3,2,1,0:T(8,128)(2,1)} %attend.1), calls=%async_computation | async-start | bytes 3670016 | tf_op jit(solution)/shard_map/all_to_all | solution.py:264
  70.8 2.4 %dynamic-slice_bitcast_fusion = (bf16[2,104,1024]{2,1,0:T(8,128)(2,1)S(1)}, bf16[2,104,1024]{2,1,0:T(8,128)(2,1)S(1)}, bf16[2,104,1024]{2,1,0:T(8,128)(2,1)S(1)}, bf16[2,104,1024]{2,1,0:T(8,128)(2,1)}) fusion(bf16[2,4,392,1024]{3,2,1,0:T(8,128)(2,1)} %bitcast.39, s32[]{:T(128)S(6)} %select_n.34, s32[]{:T(128)S(6)} %select_n.31, s32[]{:T(128)S(6)} %select_n.33, ...), kind=kLoop, calls=%fused_computation.1 | loop fusion | bytes 3407892 | tf_op jit(solution)/shard_map/reshape | solution.py:258
  73.2 3.1 %collective-permute-start.3 = (bf16[2,104,1024]{2,1,0:T(8,128)(2,1)S(1)}, bf16[2,104,1024]{2,1,0:T(8,128)(2,1)S(1)}, u32[]{:S(2)}, u32[]{:S(2)}) collective-permute-start(bf16[2,104,1024]{2,1,0:T(8,128)(2,1)S(1)} %get-tuple-element.15), channel_id=1, source_target_pairs={{0,12},{4,0},{8,4},{12,8},{1,13},{5,1},{9,5},{13,9},{2,14},{6,2},{... | collective-permute-start | bytes 1277960 | tf_op jit(solution)/shard_map/ppermute | solution.py:260
  76.3 0.9 collective-permute-start.2
  77.1 0.9 collective-permute-start.1
  78.0 25.3 %collective-permute-done.3.x3_ref = bf16[2,104,1024]{2,1,0:T(8,128)(2,1)S(1)} collective-permute-done((bf16[2,104,1024]{2,1,0:T(8,128)(2,1)S(1)}, bf16[2,104,1024]{2,1,0:T(8,128)(2,1)S(1)}, u32[]{:S(2)}, u32[]{:S(2)}) %collective-permute-start.3) | collective-permute-done | bytes 426016 | tf_op jit(solution)/shard_map/ppermute | solution.py:260
  103.3 1.5 collective-permute-done.2.x2_ref
  104.8 0.8 copy-done.3
  105.6 6.1 %collective-permute-done.1.x1_ref = bf16[2,104,1024]{2,1,0:T(8,128)(2,1)} collective-permute-done((bf16[2,104,1024]{2,1,0:T(8,128)(2,1)S(1)}, bf16[2,104,1024]{2,1,0:T(8,128)(2,1)}, u32[]{:S(2)}, u32[]{:S(2)}) %collective-permute-start.1) | collective-permute-done | bytes 426016 | tf_op jit(solution)/shard_map/ppermute | solution.py:260
  111.8 1.3 copy-done.1
  113.0 13.8 %recur.1 = (f32[4,208,1024]{2,1,0:T(8,128)}, f32[4,832,256]{2,1,0:T(8,128)}, f32[4,8,256]{2,1,0:T(8,128)}, f32[4,832,256]{2,1,0:T(8,128)}, bf16[4,104,256]{2,1,0:T(8,128)(2,1)}) custom-call(s32[1]{0:T(128)} %bitcast.place_ref, bf16[16,2,112,256]{3,2,1,0:T(8,128)(2,1)} %copy-done.1, bf16[2,104,1024]{2,1,0:T(8,128)(2,1)} %get-tuple-element.18.x0_ref, ...), custom_call_target="tpu_custom_call" | custom-call | tf_op jit(solution)/shard_map/recur/pallas_call | solution.py:269
  126.8 3.5 %collective-permute-start.4 = (bf16[4,104,256]{2,1,0:T(8,128)(2,1)}, bf16[4,104,256]{2,1,0:T(8,128)(2,1)S(1)}, u32[]{:S(2)}, u32[]{:S(2)}) collective-permute-start(bf16[4,104,256]{2,1,0:T(8,128)(2,1)} %get-tuple-element.13), channel_id=1, source_target_pairs={{0,16},{16,32},{32,48},{1,17},{17,33},{33,49},{2,18},{18,34},{34,5... | collective-permute-start | bytes 638984 | tf_op jit(solution)/shard_map/ppermute | solution.py:303
  130.4 4.4 %collective-permute-done.4.incoming_ref = bf16[4,104,256]{2,1,0:T(8,128)(2,1)S(1)} collective-permute-done((bf16[4,104,256]{2,1,0:T(8,128)(2,1)}, bf16[4,104,256]{2,1,0:T(8,128)(2,1)S(1)}, u32[]{:S(2)}, u32[]{:S(2)}) %collective-permute-start.4) | collective-permute-done | bytes 213024 | tf_op jit(solution)/shard_map/ppermute | solution.py:303
  134.8 0.7 copy-done.4
  135.5 8.1 %finish.1 = bf16[4,4,2,104,256]{4,3,2,1,0:T(8,128)(2,1)} custom-call(f32[4,832,256]{2,1,0:T(8,128)} %get-tuple-element.10.state_ref, f32[4,8,256]{2,1,0:T(8,128)} %get-tuple-element.11.decay_ref, f32[4,832,256]{2,1,0:T(8,128)} %get-tuple-element.12.open_ref, bf16[4,104,256]{2,1,0:T(8,128)(2,1)} %copy-done.4, f32[4,208,1024]{2,1,0:T(8,128)} %get-tuple-element.14.residual_ref, ...), custom_call_target="tpu_custom_call" | custom-call | tf_op jit(solution)/shard_map/finish/pallas_call | solution.py:305
  143.6 27.3 %all_to_all.10 = bf16[16,2,104,256]{3,2,1,0:T(8,128)(2,1)} all-to-all(bf16[16,2,104,256]{3,2,1,0:T(8,128)(2,1)} %bitcast.34), channel_id=1, replica_groups=mesh['clip'=2,'z'=4,'x'=4,'head'=4] {'x','head'}, dimensions={0} | all-to-all | bytes 3407872 | tf_op jit(solution)/shard_map/all_to_all | solution.py:323
  170.9 3.6 %place.1 = bf16[2,4,392,256]{3,2,1,0:T(8,128)(2,1)} custom-call(bf16[4,4,2,104,256]{4,3,2,1,0:T(8,128)(2,1)} %bitcast.35), custom_call_target="tpu_custom_call" | custom-call | tf_op jit(solution)/shard_map/place/pallas_call | solution.py:324
  (20 shorter events, 0.1 us)
Async XLA Ops:
  6.5 3.6 %copy-start = (bf16[3,1024,256]{2,1,0:T(8,128)(2,1)S(1)}, bf16[3,1024,256]{2,1,0:T(8,128)(2,1)}, u32[]{:S(2)}) copy-start(bf16[3,1024,256]{2,1,0:T(8,128)(2,1)} %param.13) | copy-start | bytes 4718596
  6.5 105.2 %all-gather.3.cloned.1.call-start = ((), (), s32[]{:S(2)}) async-start(), calls=%async_computation.2 | async-start | bytes 11796480 | tf_op jit(solution)/shard_map/all_gather | solution.py:251
  10.2 1.2 copy-start.6
  10.3 5.2 %copy-start.5 = (s32[2,1568]{1,0:T(2,128)S(1)}, s32[2,1568]{1,0:T(2,128)}, u32[]{:S(2)}) copy-start(s32[2,1568]{1,0:T(2,128)} %param.9) | copy-start | bytes 37636
  11.4 8.3 %copy-start.7 = (f32[2,256]{1,0:T(2,128)S(1)}, f32[2,256]{1,0:T(2,128)}, u32[]{:S(2)}) copy-start(f32[2,256]{1,0:T(2,128)} %param.14) | copy-start | bytes 6148
  12.0 8.2 %collective-permute-start = (s32[1]{0:T(128)}, s32[1]{0:T(128)}, u32[]{:S(2)}, u32[]{:S(2)}) collective-permute-start(s32[1]{0:T(128)} %get-tuple-element.19), channel_id=1, source_target_pairs={{0,4},{4,8},{8,12},{12,16},{16,20},{20,24},{24,28},{28,32},{32,36}... | collective-permute-start | bytes 20 | tf_op jit(solution)/shard_map/ppermute | solution.py:247
  63.4 48.3 %all-to-all-start = ((bf16[16,2,112,256]{3,2,1,0:T(8,128)(2,1)}), bf16[16,2,112,256]{3,2,1,0:T(8,128)(2,1)S(1)}, u32[]{:S(2)}, u32[]{:S(2)}) async-start(bf16[16,2,112,256]{3,2,1,0:T(8,128)(2,1)} %attend.1), calls=%async_computation | async-start | bytes 3670016 | tf_op jit(solution)/shard_map/all_to_all | solution.py:264
  73.2 30.1 %collective-permute-start.3 = (bf16[2,104,1024]{2,1,0:T(8,128)(2,1)S(1)}, bf16[2,104,1024]{2,1,0:T(8,128)(2,1)S(1)}, u32[]{:S(2)}, u32[]{:S(2)}) collective-permute-start(bf16[2,104,1024]{2,1,0:T(8,128)(2,1)S(1)} %get-tuple-element.15), channel_id=1, source_target_pairs={{0,12},{4,0},{8,4},{12,8},{1,13},{5,1},{9,5},{13,9},{2,14},{6,2},{... | collective-permute-start | bytes 1277960 | tf_op jit(solution)/shard_map/ppermute | solution.py:260
  76.3 28.6 %collective-permute-start.2 = (bf16[2,104,1024]{2,1,0:T(8,128)(2,1)S(1)}, bf16[2,104,1024]{2,1,0:T(8,128)(2,1)S(1)}, u32[]{:S(2)}, u32[]{:S(2)}) collective-permute-start(bf16[2,104,1024]{2,1,0:T(8,128)(2,1)S(1)} %get-tuple-element.16), channel_id=1, source_target_pairs={{0,8},{4,12},{8,0},{12,4},{1,9},{5,13},{9,1},{13,5},{2,10},{6,14},... | collective-permute-start | bytes 1277960 | tf_op jit(solution)/shard_map/ppermute | solution.py:260
  77.1 34.6 %collective-permute-start.1 = (bf16[2,104,1024]{2,1,0:T(8,128)(2,1)S(1)}, bf16[2,104,1024]{2,1,0:T(8,128)(2,1)}, u32[]{:S(2)}, u32[]{:S(2)}) collective-permute-start(bf16[2,104,1024]{2,1,0:T(8,128)(2,1)S(1)} %get-tuple-element.17), channel_id=1, source_target_pairs={{0,4},{4,8},{8,12},{12,0},{1,5},{5,9},{9,13},{13,1},{2,6},{6,10},{... | collective-permute-start | bytes 1277960 | tf_op jit(solution)/shard_map/ppermute | solution.py:260
  103.3 1.5 copy-start.2
  104.8 0.8 copy-start.3
  111.7 1.3 copy-start.1
  126.8 7.9 %collective-permute-start.4 = (bf16[4,104,256]{2,1,0:T(8,128)(2,1)}, bf16[4,104,256]{2,1,0:T(8,128)(2,1)S(1)}, u32[]{:S(2)}, u32[]{:S(2)}) collective-permute-start(bf16[4,104,256]{2,1,0:T(8,128)(2,1)} %get-tuple-element.13), channel_id=1, source_target_pairs={{0,16},{16,32},{32,48},{1,17},{17,33},{33,49},{2,18},{18,34},{34,5... | collective-permute-start | bytes 638984 | tf_op jit(solution)/shard_map/ppermute | solution.py:303
  134.8 0.7 copy-start.4
Sparse Core Ops, SparseCore 0:
  11.6 60.5 all-gather.2

commit v2 on v1

--- a/solution.py
+++ b/solution.py
@@ -22,7 +22,7 @@
 EPSILON = 1e-06
 F32 = jnp.float32
 BF16 = jnp.bfloat16
-LIMIT = 60 * 1024 * 1024
+LIMIT = 40 * 1024 * 1024
 
 
 def dot(left, right):
@@ -37,7 +37,38 @@
     return values * lax.rsqrt(jnp.mean(values * values, axis=-1, keepdims=True) + EPSILON)
 
 
-def attend_kernel(x_ref, column_ref, row_ref, decay_ref, continues_ref, weight_ref, out_ref, normed, qkv, arranged, mixed):
+def pack_kernel(place_ref, tokens_ref, mix_ref, recur_ref, last_ref, packed_ref, *rest):
+    block_refs, (packed, blocks, sems, out_sems) = rest[:4], rest[4:]
+    c, x, h = place_ref[0], place_ref[1], place_ref[2]
+    copies = []
+
+    def copy(source, through, target):
+        i = len(copies)
+        inward = pltpu.make_async_copy(source, through, sems.at[i])
+        copies.append((inward, pltpu.make_async_copy(through, target, out_sems.at[i])))
+        inward.start()
+
+    def pack(source, rows):
+        copy(source, packed.at[rows, :], packed_ref.at[rows, :])
+
+    for q in range(2):
+        columns = pl.ds(pl.multiple_of(c * (2 * C) + q * C, C), C)
+        pack(mix_ref.at[:, columns], slice(q * C, (q + 1) * C))
+        pack(last_ref.at[:, columns], slice((8 + q) * C, (9 + q) * C))
+    for i in range(3):
+        half = pl.ds(pl.multiple_of(c * (D // 2), D // 2), D // 2)
+        pack(recur_ref.at[i, half, :], slice((i + 1) * D // 2, (i + 2) * D // 2))
+    for s, block_ref in enumerate(block_refs):
+        part = tokens_ref.at[:, lax.rem(x + s, 4), pl.ds(pl.multiple_of(h * STRIDE, 16), SHARE), :]
+        copy(part, blocks.at[s], block_ref)
+    for inward, outward in copies:
+        inward.wait()
+        outward.start()
+    for inward, outward in copies:
+        outward.wait()
+
+
+def attend_kernel(x_ref, order_ref, decay_ref, clip_ref, weight_ref, out_ref, normed, qkv, arranged, mixed):
     step = 112
 
     def norm_step(i, carry):
@@ -53,16 +84,14 @@
             rows = slice(i * half, (i + 1) * half)
             qkv[rows, k * C : (k + 1) * C] = dot(normed[rows, :], weight_ref[k]).astype(BF16)
 
-    part = 512
-
-    def arrange_step(i, carry):
-        rows = pl.ds(pl.multiple_of(i * part, part), part)
-        lanes = lax.broadcasted_iota(jnp.int32, (part, TOK), 1)
-        pick = jnp.where(lanes == column_ref[0, rows, :], 1.0, 0.0).astype(BF16)
-        arranged[rows, :] = dot(pick, qkv[...]).astype(BF16)
-        return carry
-
-    lax.fori_loop(0, ROWS // part, arrange_step, 0)
+    lanes = lax.broadcasted_iota(jnp.int32, (128, TOK), 1)
+    columns = jnp.transpose(order_ref[0])
+    for i in range(ROWS // 512):
+        pick = jnp.concatenate(
+            [jnp.where(lanes == columns[:, j : j + 1], 1.0, 0.0).astype(BF16) for j in range(4 * i, 4 * i + 4)],
+            axis=0,
+        )
+        arranged[i * 512 : (i + 1) * 512, :] = dot(pick, qkv[...]).astype(BF16)
 
     lane_head = lax.broadcasted_iota(jnp.int32, (SLOT, C), 1) // HEAD
     own = [lane_head == h for h in range(4)]
@@ -103,21 +132,26 @@
 
     lax.fori_loop(0, WINDOWS // group, window_step, 0)
 
-    decay = decay_ref[0]
+    f = pl.program_id(0)
+    decay = decay_ref[pl.ds(f, 1), :]
+    clip = clip_ref[f].astype(F32)
     high = decay.astype(BF16).astype(F32)
     middle = (decay - high).astype(BF16).astype(F32)
     index = lax.broadcasted_iota(jnp.int32, (8, C), 0)
     extra = jnp.where(
         index == 0,
         high,
-        jnp.where(index == 1, middle, jnp.where(index == 2, (decay - high) - middle, continues_ref[0])),
+        jnp.where(index == 1, middle, jnp.where(index == 2, (decay - high) - middle, clip)),
     ).astype(BF16)
 
     def restore_step(i, carry):
-        r = lax.broadcasted_iota(jnp.int32, (4 * SHARE, ROWS), 0)
+        r = lax.broadcasted_iota(jnp.int32, (4 * SHARE, 128), 0)
         late = jnp.where(r >= SHARE, 8, 0) + jnp.where(r >= 2 * SHARE, 8, 0) + jnp.where(r >= 3 * SHARE, 8, 0)
         position = r - late + i * QUARTER
-        pick = jnp.where(position == row_ref[0], 1.0, 0.0).astype(BF16)
+        pick = jnp.concatenate(
+            [jnp.where(position == order_ref[0, j : j + 1, :], 1.0, 0.0).astype(BF16) for j in range(ROWS // 128)],
+            axis=1,
+        )
         result = dot(pick, mixed[...])
         for h in range(4):
             out_ref[4 * i + h, 0, :SHARE, :] = result[h * SHARE : (h + 1) * SHARE].astype(BF16)
@@ -127,22 +161,21 @@
     lax.fori_loop(0, 4, restore_step, 0)
 
 
-def attend(tokens, window_order, frame_decay, continues, weight):
+def attend(tokens, window_order, frame_decay, clip_id, weight):
     padded = jnp.pad(
         window_order.reshape(FRAMES, WINDOWS, WINDOW),
         ((0, 0), (0, 0), (0, SLOT - WINDOW)),
         constant_values=-1,
-    ).reshape(FRAMES, ROWS)
+    ).reshape(FRAMES, ROWS // 128, 128)
     return pl.pallas_call(
         attend_kernel,
         grid=(FRAMES,),
         in_specs=[
             pl.BlockSpec((1, TOK, D), lambda f: (f, 0, 0)),
-            pl.BlockSpec((1, ROWS, 1), lambda f: (f, 0, 0)),
-            pl.BlockSpec((1, 1, ROWS), lambda f: (f, 0, 0)),
-            pl.BlockSpec((1, 1, C), lambda f: (f, 0, 0)),
-            pl.BlockSpec((1, 1, C), lambda f: (f, 0, 0)),
-            pl.BlockSpec((3, D, C), lambda f: (0, 0, 0)),
+            pl.BlockSpec((1, ROWS // 128, 128), lambda f: (f, 0, 0)),
+            pl.BlockSpec((FRAMES, C), lambda f: (0, 0)),
+            pl.BlockSpec(memory_space=pltpu.SMEM),
+            pl.BlockSpec((3, D, C), lambda f: (0, 0, 0), pipeline_mode=pl.Buffered(1)),
         ],
         out_specs=pl.BlockSpec((16, 1, SENT, C), lambda f: (0, f, 0, 0)),
         out_shape=jax.ShapeDtypeStruct((16, FRAMES, SENT, C), BF16),
@@ -159,7 +192,7 @@
             transcendentals=FRAMES * ROWS * C,
         ),
         name="attend",
-    )(tokens, padded[:, :, None], padded[:, None, :], frame_decay[:, None, :], continues, weight)
+    )(tokens, padded, frame_decay, clip_id, weight)
 
 
 def recur_kernel(
@@ -197,17 +230,23 @@
     opening = project(open_ref)
     open_out_ref[0] = opening * jax.nn.sigmoid(opening)
     state = jnp.zeros((SHARE, C), F32)
+    first = before = None
     decay = jnp.ones((1, C), F32)
     for f in range(4 * FRAMES):
         extra = att_ref[(f // 2) * 4 + h, f % 2, SHARE:, :].astype(F32)
         retain = jnp.exp(extra[0:1] + extra[1:2] + extra[2:3])
-        factor = retain * extra[3:4]
+        clip = extra[3:4]
+        factor = retain * jnp.where(clip == before, 1.0, 0.0) if f else retain
+        first = first if f else clip
+        before = clip
         drive = jnp.sqrt(1.0 - retain * retain)
         decay = factor * decay
         state = factor * state + drive * driven[f * SHARE : (f + 1) * SHARE]
         state_ref[0, f * SHARE : (f + 1) * SHARE, :] = state
         decay_ref[0, f : f + 1, :] = decay
-    last_ref[0] = state.astype(BF16)
+    last_ref[0, :SHARE, :] = state.astype(BF16)
+    last_ref[0, SHARE:, :] = jnp.broadcast_to(before, (8, C)).astype(BF16)
+    decay_ref[0, 8:, :] = jnp.broadcast_to(first, (8, C))
 
 
 def finish_kernel(state_ref, decay_ref, open_ref, incoming_ref, residual_ref, weight_ref, out_ref, rows):
@@ -216,7 +255,8 @@
     @pl.when(n == 0)
     def _():
         for k in range(4):
-            incoming = incoming_ref[k].astype(F32)
+            continues = incoming_ref[k, SHARE:, :].astype(F32) == decay_ref[k, 8:, :]
+            incoming = incoming_ref[k, :SHARE, :].astype(F32) * jnp.where(continues, 1.0, 0.0)[:1]
             for f in range(4 * FRAMES):
                 piece = slice(f * SHARE, (f + 1) * SHARE)
                 state = state_ref[k, piece, :] + decay_ref[k, f : f + 1, :] * incoming
@@ -228,42 +268,52 @@
     out_ref[...] = total.reshape(4, 1, FRAMES, SHARE, C).astype(BF16)
 
 
-def place_kernel(in_ref, out_ref):
-    for k in range(4):
-        size = STRIDE if k < 3 else SHARE
-        for f in range(FRAMES):
-            out_ref[f, 0, k * STRIDE : k * STRIDE + size, :] = in_ref[0, k, f, :size, :]
+def place_kernel(in_ref, out_ref, held, sems, out_sems):
+    copies = []
+    for x in range(4):
+        for k in range(4):
+            size = STRIDE if k < 3 else SHARE
+            i = len(copies)
+            through = held.at[i, :, :size, :]
+            inward = pltpu.make_async_copy(in_ref.at[x, k, :, :size, :], through, sems.at[i])
+            target = out_ref.at[:, x, k * STRIDE : k * STRIDE + size, :]
+            copies.append((inward, pltpu.make_async_copy(through, target, out_sems.at[i])))
+            inward.start()
+    for inward, outward in copies:
+        inward.wait()
+        outward.start()
+    for inward, outward in copies:
+        outward.wait()
 
 
 def per_device(tokens, window_order, clip_id, attend_weight, attend_out, recur_weight, frame_decay, recur_out):
     c, z, x, h = (lax.axis_index(name) for name in ("clip", "z", "x", "head"))
 
-    def column_blocks(weight):
-        blocks = weight.reshape(C, 4, C).transpose(1, 0, 2)
-        return lax.dynamic_slice_in_dim(blocks, 2 * c, 2, 0).reshape(2 * C, C)
-
-    half = lax.dynamic_slice_in_dim(recur_weight, c * (D // 2), D // 2, 1).reshape(3 * D // 2, C)
-    packed = jnp.concatenate([column_blocks(attend_out), half, column_blocks(recur_out)], axis=0)
-    before = lax.ppermute(clip_id[1:], ("z", "x"), [(i, i + 1) for i in range(15)])
-    continues = (clip_id == jnp.concatenate([before, clip_id[:1]])).astype(F32)
-    continues = continues * jnp.where((jnp.arange(FRAMES) > 0) | (z > 0) | (x > 0), 1.0, 0.0)
-    continues = jnp.broadcast_to(continues[:, None, None], (FRAMES, 1, C))
+    here = pl.BlockSpec(memory_space=pl.ANY)
+    packed, *blocks = pl.pallas_call(
+        pack_kernel,
+        in_specs=[pl.BlockSpec(memory_space=pltpu.SMEM), here, here, here, here],
+        out_specs=[here] * 5,
+        out_shape=[jax.ShapeDtypeStruct((5 * D // 2, C), BF16)]
+        + [jax.ShapeDtypeStruct((FRAMES, SHARE, D), BF16)] * 4,
+        scratch_shapes=[
+            pltpu.VMEM((5 * D // 2, C), BF16),
+            pltpu.VMEM((4, FRAMES, SHARE, D), BF16),
+            pltpu.SemaphoreType.DMA((11,)),
+            pltpu.SemaphoreType.DMA((11,)),
+        ],
+        name="pack",
+    )(jnp.stack([c, x, h]), tokens.reshape(FRAMES, 4, QUARTER, D), attend_out, recur_weight, recur_out)
     weights = lax.all_gather(packed, ("clip", "head"), axis=0).reshape(2, 4, 5 * D // 2, C)
-
-    quarters = tokens.reshape(FRAMES, 4, QUARTER, D)
-    moved = []
-    for s in range(4):
-        block = lax.dynamic_slice(
-            quarters, (0, lax.rem(x + s, 4), h * STRIDE, 0), (FRAMES, 1, SHARE, D)
-        ).reshape(FRAMES, SHARE, D)
-        if s:
-            block = lax.ppermute(block, "x", [(i, (i + s) % 4) for i in range(4)])
-        moved.append(block)
-
-    mixed = attend(tokens, window_order, frame_decay, continues, attend_weight)
+    moved = [
+        lax.ppermute(blocks[s], "x", [(i, (i + s) % 4) for i in range(4)]) if s else blocks[0] for s in range(4)
+    ]
+
+    mixed = attend(tokens, window_order, frame_decay, clip_id, attend_weight)
+    mixed, *moved = lax.optimization_barrier((mixed, *moved))
     mixed = lax.all_to_all(mixed, ("x", "head"), 0, 0)
 
-    whole = lambda shape: pl.BlockSpec(shape, lambda n: (0,) * len(shape))
+    whole = lambda shape: pl.BlockSpec(shape, lambda n: (0,) * len(shape), pipeline_mode=pl.Buffered(1))
     span = D // 2
     wide = 8 * SHARE
     residual, state, decay, opened, last = pl.pallas_call(
@@ -282,18 +332,18 @@
             pl.BlockSpec((2, 1, span, C), lambda n: (0, n, 3, 0)),
         ],
         out_specs=[
-            whole((4, FRAMES * SHARE, D)),
+            pl.BlockSpec((4, FRAMES * SHARE, D), lambda n: (0, 0, 0)),
             pl.BlockSpec((1, wide, C), lambda n: (n, 0, 0)),
-            pl.BlockSpec((1, 8, C), lambda n: (n, 0, 0)),
+            pl.BlockSpec((1, 16, C), lambda n: (n, 0, 0)),
             pl.BlockSpec((1, wide, C), lambda n: (n, 0, 0)),
-            pl.BlockSpec((1, SHARE, C), lambda n: (n, 0, 0)),
+            pl.BlockSpec((1, SENT, C), lambda n: (n, 0, 0)),
         ],
         out_shape=[
             jax.ShapeDtypeStruct((4, FRAMES * SHARE, D), F32),
             jax.ShapeDtypeStruct((4, wide, C), F32),
-            jax.ShapeDtypeStruct((4, 8, C), F32),
+            jax.ShapeDtypeStruct((4, 16, C), F32),
             jax.ShapeDtypeStruct((4, wide, C), F32),
-            jax.ShapeDtypeStruct((4, SHARE, C), BF16),
+            jax.ShapeDtypeStruct((4, SENT, C), BF16),
         ],
         scratch_shapes=[pltpu.VMEM((4, FRAMES * SHARE, D), BF16)],
         compiler_params=pltpu.CompilerParams(vmem_limit_bytes=LIMIT),
@@ -307,9 +357,9 @@
         grid=(4,),
         in_specs=[
             whole((4, wide, C)),
-            whole((4, 8, C)),
+            whole((4, 16, C)),
             whole((4, wide, C)),
-            whole((4, SHARE, C)),
+            whole((4, SENT, C)),
             pl.BlockSpec((4, FRAMES * SHARE, C), lambda n: (0, 0, n)),
             pl.BlockSpec((1, 4, C, C), lambda n: (n // 2, 0, 8 + n % 2, 0)),
         ],
@@ -323,10 +373,14 @@
     result = lax.all_to_all(result.reshape(16, FRAMES, SHARE, C), ("x", "head"), 0, 0)
     placed = pl.pallas_call(
         place_kernel,
-        grid=(4,),
-        in_specs=[pl.BlockSpec((1, 4, FRAMES, SHARE, C), lambda n: (n, 0, 0, 0, 0))],
-        out_specs=pl.BlockSpec((FRAMES, 1, QUARTER, C), lambda n: (0, n, 0, 0)),
+        in_specs=[here],
+        out_specs=here,
         out_shape=jax.ShapeDtypeStruct((FRAMES, 4, QUARTER, C), BF16),
+        scratch_shapes=[
+            pltpu.VMEM((16, FRAMES, SHARE, C), BF16),
+            pltpu.SemaphoreType.DMA((16,)),
+            pltpu.SemaphoreType.DMA((16,)),
+        ],
         name="place",
     )(result.reshape(4, 4, FRAMES, SHARE, C))
     return placed.reshape(FRAMES, TOK, C)

time: 182 us -> 155 us (0.85)
  blocking collectives: 27.3 us -> 62 us
  waiting for transfers between devices: 37.4 us -> 9.75 us
  local copies, waits for them, and re-layouts: 14.8 us -> 3.02 us
  starting transfers between devices: 19.1 us -> 9.2 us
  Pallas kernels: 66.6 us -> 56.8 us
  other arithmetic: 2.49 us -> 0.62 us
    ppermute x4 -> x3, waiting for transfers between devices: 33 us -> 0.01 us  [per_device(): lax.ppermute(blocks[s], 'x', [(i, (i + s) % 4) for i in range(4)])]
    all_to_all x0 -> x1, blocking collectives: none -> 32.7 us  [per_device(): mixed = lax.all_to_all(mixed, ('x', 'head'), 0, 0)]
    all_to_all x1 -> x0, starting transfers between devices: 7.4 us -> none  [per_device(): mixed = lax.all_to_all(mixed, ('x', 'head'), 0, 0)]
    pallas_call x1, Pallas kernels: 41.1 us -> 35.3 us  [attend(): pl.pallas_call(attend_kernel, grid=(FRAMES,), in_specs=[pl.BlockSpec((1,...]
    reshape x3 -> x1, local copies, waits for them, and re-layouts: 5.35 us -> 0.07 us  [attend(): padded = jnp.pad(window_order.reshape(FRAMES, WINDOWS, WINDOW), ((0, 0),...]
    another operation x2 -> x0, local copies, waits for them, and re-layouts: 4.1 us -> none  [the longest x1 3.42 us: attend(): padded[:, :, None]]
    all_gather x1, waiting for transfers between devices: 0.01 us -> 3.54 us  [per_device(): lax.all_gather(packed, ('clip', 'head'), axis=0)]
    pallas_call x1, Pallas kernels: 13.8 us -> 10.4 us  [per_device(): pl.pallas_call(recur_kernel, grid=(4,), in_specs=[pl.BlockSpec(memory_spa...]
  transfers between devices with their start and end apart: 7 -> 5, of which waited for: 4 -> 2; matrix products, arithmetic and copies ran while one was open for 5% -> 0% of each run, Pallas kernels for 23% -> 23%
where the time goes in v2:
time: 155 us
  blocking collectives  62 us (40%)
  Pallas kernels  56.8 us (37%)
  between operations  13.5 us (9%)
  waiting for transfers between devices  9.75 us (6%)
  starting transfers between devices  9.2 us (6%)
  local copies, waits for them, and re-layouts  3.02 us (2%)
    pallas_call x1, Pallas kernels, attend(): pl.pallas_call(attend_kernel, grid=(FRAMES,), in_specs=[pl.BlockSpec((1,...  35.3 us
    all_to_all x1, blocking collectives, per_device(): mixed = lax.all_to_all(mixed, ('x', 'head'), 0, 0)  32.7 us
    all_to_all x1, blocking collectives, per_device(): lax.all_to_all(result.reshape(16, FRAMES, SHARE, C), ('x', 'head'), 0, 0)  29.3 us
    pallas_call x1, Pallas kernels, per_device(): pl.pallas_call(recur_kernel, grid=(4,), in_specs=[pl.BlockSpec(memory_spa...  10.4 us
    ppermute x1, waiting for transfers between devices, per_device(): incoming = lax.ppermute(last, 'z', [(i, i + 1) for i in range(3)])  6.19 us
    ppermute x3, starting transfers between devices, per_device(): lax.ppermute(blocks[s], 'x', [(i, (i + s) % 4) for i in range(4)])  5.72 us
    pallas_call x1, Pallas kernels, per_device(): pl.pallas_call(finish_kernel, grid=(4,), in_specs=[whole((4, wide, C)), w...  4.83 us
    pallas_call x1, Pallas kernels, per_device(): pl.pallas_call(pack_kernel, in_specs=[pl.BlockSpec(memory_space=pltpu.SME...  3.83 us
  transfers between devices with their start and end apart: 5, of which 2 were waited for; matrix products, arithmetic and copies ran while one was open for 0% of the time, Pallas kernels for 23%

profile of v2, /device:TPU:32, one launch (start us, length us, event | category | flops | bytes accessed | tf_op | source)
XLA Modules:
  0.0 154.9 jit_solution(16513491977791624279)
XLA Ops:
  6.5 0.0 all-gather.3.cloned.1.call-start
  6.5 0.6 pad_add_fusion.place_ref
  7.2 0.0 copy-start.5
  7.2 0.0 copy-start.2
  7.2 0.0 copy-start.3
  7.2 3.8 %pack.1 = (bf16[2560,256]{1,0:T(8,128)(2,1)}, bf16[2,104,1024]{2,1,0:T(8,128)(2,1)}, bf16[2,104,1024]{2,1,0:T(8,128)(2,1)}, bf16[2,104,1024]{2,1,0:T(8,128)(2,1)}, bf16[2,104,1024]{2,1,0:T(8,128)(2,1)}) custom-call(s32[3]{0:T(128)} %pad_add_fusion.place_ref, bf16[2,4,392,1024]{3,2,1,0:T(8,128)(2,1)} %bitcast.9, bf16[256,1024]{1,0:T(8,128)(2,1)} %mix_ref.1, ...), custom_call_target="tpu_custom_call" | custom-call | tf_op jit(solution)/shard_map/pack/pallas_call | solution.py:293
  11.0 0.0 all-gather.3.cloned.1.call-update
  11.0 1.6 %collective-permute-start = (bf16[2,104,1024]{2,1,0:T(8,128)(2,1)}, bf16[2,104,1024]{2,1,0:T(8,128)(2,1)S(1)}, u32[]{:S(2)}, u32[]{:S(2)}) collective-permute-start(bf16[2,104,1024]{2,1,0:T(8,128)(2,1)} %get-tuple-element.21), channel_id=1, source_target_pairs={{0,4},{4,8},{8,12},{12,0},{1,5},{5,9},{9,13},{13,1},{2,6},{6,10},{... | collective-permute-start | bytes 1277960 | tf_op jit(solution)/shard_map/ppermute | solution.py:309
  12.6 2.7 %collective-permute-start.1 = (bf16[2,104,1024]{2,1,0:T(8,128)(2,1)}, bf16[2,104,1024]{2,1,0:T(8,128)(2,1)S(1)}, u32[]{:S(2)}, u32[]{:S(2)}) collective-permute-start(bf16[2,104,1024]{2,1,0:T(8,128)(2,1)} %get-tuple-element.22), channel_id=1, source_target_pairs={{0,8},{4,12},{8,0},{12,4},{1,9},{5,13},{9,1},{13,5},{2,10},{6,14},... | collective-permute-start | bytes 1277960 | tf_op jit(solution)/shard_map/ppermute | solution.py:309
  15.3 1.4 collective-permute-start.2
  16.8 0.0 copy-done.5
  16.8 0.1 reshape.21
  16.9 0.1 reshape.22.order_ref
  17.0 0.0 copy-done.2
  17.0 0.0 copy-done.3
  17.0 0.0 copy-done.4
  17.0 0.0 copy-start
  17.0 2.8 %copy-done = bf16[2,1568,1024]{2,1,0:T(8,128)(2,1)S(1)} copy-done((bf16[2,1568,1024]{2,1,0:T(8,128)(2,1)S(1)}, bf16[2,1568,1024]{2,1,0:T(8,128)(2,1)}, u32[]{:S(2)}) %copy-start) | copy-done | bytes 6422552
  19.8 35.3 %attend.1 = bf16[16,2,112,256]{3,2,1,0:T(8,128)(2,1)S(1)} custom-call(bf16[2,1568,1024]{2,1,0:T(8,128)(2,1)S(1)} %copy-done, s32[2,16,128]{2,1,0:T(8,128)S(1)} %reshape.22.order_ref, f32[2,256]{1,0:T(2,128)S(1)} %copy-done.3, s32[2]{0:T(128)S(1)} %copy-done.4, bf16[3,1024,256]{2,1,0:T(8,128)(2,1)S(1)} %copy-done.2), custom_call_target="tpu_custom_call" | custom-call | flops 20233322496 | bytes 12845056 | tf_op jit(solution)/shard_map/attend/pallas_call | solution.py:170
  55.1 0.0 collective-permute-done.x1_ref
  55.1 0.0 collective-permute-done.1.x2_ref
  55.1 0.0 collective-permute-done.2.x3_ref
  55.1 0.0 copy-start.1
  55.1 32.7 %all_to_all.10.att_ref = bf16[16,2,112,256]{3,2,1,0:T(8,128)(2,1)S(1)} all-to-all(bf16[16,2,112,256]{3,2,1,0:T(8,128)(2,1)S(1)} %attend.1), channel_id=1, replica_groups=mesh['clip'=2,'z'=4,'x'=4,'head'=4] {'x','head'}, dimensions={0} | all-to-all | bytes 3670016 | tf_op jit(solution)/shard_map/all_to_all | solution.py:314
  87.9 3.5 %all-gather.3.cloned.1.call-done = bf16[20480,256]{1,0:T(8,128)(2,1)} async-done(((bf16[2560,256]{1,0:T(8,128)(2,1)}), bf16[20480,256]{1,0:T(8,128)(2,1)}) %all-gather.3.cloned.1.call-update) | async-done | bytes 10485776 | tf_op jit(solution)/shard_map/all_gather | solution.py:307
  91.4 0.0 copy-done.1
  91.4 10.4 %recur.1 = (f32[4,208,1024]{2,1,0:T(8,128)S(1)}, f32[4,832,256]{2,1,0:T(8,128)S(1)}, f32[4,16,256]{2,1,0:T(8,128)S(1)}, f32[4,832,256]{2,1,0:T(8,128)S(1)}, bf16[4,112,256]{2,1,0:T(8,128)(2,1)S(1)}) custom-call(s32[1]{0:T(128)} %bitcast.place_ref, bf16[16,2,112,256]{3,2,1,0:T(8,128)(2,1)S(1)} %all_to_all.10.att_ref, bf16[2,104,1024]{2,1,0:T(8,128)(2,1)S(1)} %copy-done.1, ...), custom_call_target="tpu_custom_call" | custom-call | tf_op jit(solution)/shard_map/recur/pallas_call | solution.py:319
  101.9 3.5 %collective-permute-start.3 = (bf16[4,112,256]{2,1,0:T(8,128)(2,1)S(1)}, bf16[4,112,256]{2,1,0:T(8,128)(2,1)S(1)}, u32[]{:S(2)}, u32[]{:S(2)}) collective-permute-start(bf16[4,112,256]{2,1,0:T(8,128)(2,1)S(1)} %get-tuple-element.33), channel_id=1, source_target_pairs={{0,16},{16,32},{32,48},{1,17},{17,33},{33,49},{2,18},{18,34},{34,5... | collective-permute-start | bytes 688136 | tf_op jit(solution)/shard_map/ppermute | solution.py:353
  105.3 6.2 %collective-permute-done.3.incoming_ref = bf16[4,112,256]{2,1,0:T(8,128)(2,1)S(1)} collective-permute-done((bf16[4,112,256]{2,1,0:T(8,128)(2,1)S(1)}, bf16[4,112,256]{2,1,0:T(8,128)(2,1)S(1)}, u32[]{:S(2)}, u32[]{:S(2)}) %collective-permute-start.3) | collective-permute-done | bytes 229408 | tf_op jit(solution)/shard_map/ppermute | solution.py:353
  111.5 4.8 %finish.1 = bf16[4,4,2,104,256]{4,3,2,1,0:T(8,128)(2,1)S(1)} custom-call(f32[4,832,256]{2,1,0:T(8,128)S(1)} %get-tuple-element.30.state_ref, f32[4,16,256]{2,1,0:T(8,128)S(1)} %get-tuple-element.31.decay_ref, f32[4,832,256]{2,1,0:T(8,128)S(1)} %get-tuple-element.32.open_ref, bf16[4,112,256]{2,1,0:T(8,128)(2,1)S(1)} %collective-permute-done.3.incoming_ref, ...), custom_call_target="tpu_custom_call" | custom-call | tf_op jit(solution)/shard_map/finish/pallas_call | solution.py:355
  116.4 29.3 %all_to_all.11 = bf16[16,2,104,256]{3,2,1,0:T(8,128)(2,1)} all-to-all(bf16[16,2,104,256]{3,2,1,0:T(8,128)(2,1)S(1)} %bitcast.8), channel_id=1, replica_groups=mesh['clip'=2,'z'=4,'x'=4,'head'=4] {'x','head'}, dimensions={0} | all-to-all | bytes 3407872 | tf_op jit(solution)/shard_map/all_to_all | solution.py:373
  145.7 2.4 %place.1 = bf16[2,4,392,256]{3,2,1,0:T(8,128)(2,1)} custom-call(bf16[4,4,2,104,256]{4,3,2,1,0:T(8,128)(2,1)} %bitcast.15), custom_call_target="tpu_custom_call" | custom-call | tf_op jit(solution)/shard_map/place/pallas_call | solution.py:374
  (2 shorter events, 0.0 us)
Async XLA Ops:
  6.5 84.9 %all-gather.3.cloned.1.call-start = ((), (), s32[]{:S(2)}) async-start(), calls=%async_computation.2 | async-start | bytes 11796480 | tf_op jit(solution)/shard_map/all_gather | solution.py:307
  7.2 9.6 %copy-start.5 = (s32[2,1568]{1,0:T(2,128)S(1)}, s32[2,1568]{1,0:T(2,128)}, u32[]{:S(2)}) copy-start(s32[2,1568]{1,0:T(2,128)} %param.9) | copy-start | bytes 37636
  7.2 9.8 %copy-start.2 = (bf16[3,1024,256]{2,1,0:T(8,128)(2,1)S(1)}, bf16[3,1024,256]{2,1,0:T(8,128)(2,1)}, u32[]{:S(2)}) copy-start(bf16[3,1024,256]{2,1,0:T(8,128)(2,1)} %weight_ref.1) | copy-start | bytes 4718596
  7.2 9.8 %copy-start.3 = (f32[2,256]{1,0:T(2,128)S(1)}, f32[2,256]{1,0:T(2,128)}, u32[]{:S(2)}) copy-start(f32[2,256]{1,0:T(2,128)} %decay_ref.1) | copy-start | bytes 6148
  7.2 9.8 %copy-start.4 = (s32[2]{0:T(128)S(1)}, s32[2]{0:T(128)}, u32[]{:S(2)}) copy-start(s32[2]{0:T(128)} %clip_ref.1) | copy-start | bytes 28
  11.0 44.1 %collective-permute-start = (bf16[2,104,1024]{2,1,0:T(8,128)(2,1)}, bf16[2,104,1024]{2,1,0:T(8,128)(2,1)S(1)}, u32[]{:S(2)}, u32[]{:S(2)}) collective-permute-start(bf16[2,104,1024]{2,1,0:T(8,128)(2,1)} %get-tuple-element.21), channel_id=1, source_target_pairs={{0,4},{4,8},{8,12},{12,0},{1,5},{5,9},{9,13},{13,1},{2,6},{6,10},{... | collective-permute-start | bytes 1277960 | tf_op jit(solution)/shard_map/ppermute | solution.py:309
  12.6 42.5 %collective-permute-start.1 = (bf16[2,104,1024]{2,1,0:T(8,128)(2,1)}, bf16[2,104,1024]{2,1,0:T(8,128)(2,1)S(1)}, u32[]{:S(2)}, u32[]{:S(2)}) collective-permute-start(bf16[2,104,1024]{2,1,0:T(8,128)(2,1)} %get-tuple-element.22), channel_id=1, source_target_pairs={{0,8},{4,12},{8,0},{12,4},{1,9},{5,13},{9,1},{13,5},{2,10},{6,14},... | collective-permute-start | bytes 1277960 | tf_op jit(solution)/shard_map/ppermute | solution.py:309
  15.3 39.8 %collective-permute-start.2 = (bf16[2,104,1024]{2,1,0:T(8,128)(2,1)}, bf16[2,104,1024]{2,1,0:T(8,128)(2,1)S(1)}, u32[]{:S(2)}, u32[]{:S(2)}) collective-permute-start(bf16[2,104,1024]{2,1,0:T(8,128)(2,1)} %get-tuple-element.23), channel_id=1, source_target_pairs={{0,12},{4,0},{8,4},{12,8},{1,13},{5,1},{9,5},{13,9},{2,14},{6,2},{... | collective-permute-start | bytes 1277960 | tf_op jit(solution)/shard_map/ppermute | solution.py:309
  17.0 2.8 %copy-start = (bf16[2,1568,1024]{2,1,0:T(8,128)(2,1)S(1)}, bf16[2,1568,1024]{2,1,0:T(8,128)(2,1)}, u32[]{:S(2)}) copy-start(bf16[2,1568,1024]{2,1,0:T(8,128)(2,1)} %x_ref.1) | copy-start | bytes 19267588
  55.1 36.3 %copy-start.1 = (bf16[2,104,1024]{2,1,0:T(8,128)(2,1)S(1)}, bf16[2,104,1024]{2,1,0:T(8,128)(2,1)}, u32[]{:S(2)}) copy-start(bf16[2,104,1024]{2,1,0:T(8,128)(2,1)} %get-tuple-element.25.x0_ref) | copy-start | bytes 1277956
  101.9 9.7 %collective-permute-start.3 = (bf16[4,112,256]{2,1,0:T(8,128)(2,1)S(1)}, bf16[4,112,256]{2,1,0:T(8,128)(2,1)S(1)}, u32[]{:S(2)}, u32[]{:S(2)}) collective-permute-start(bf16[4,112,256]{2,1,0:T(8,128)(2,1)S(1)} %get-tuple-element.33), channel_id=1, source_target_pairs={{0,16},{16,32},{32,48},{1,17},{17,33},{33,49},{2,18},{18,34},{34,5... | collective-permute-start | bytes 688136 | tf_op jit(solution)/shard_map/ppermute | solution.py:353
Sparse Core Ops, SparseCore 0:
  11.2 80.2 all-gather.2

commit v3 on v2

--- a/solution.py
+++ b/solution.py
@@ -23,6 +23,7 @@
 F32 = jnp.float32
 BF16 = jnp.bfloat16
 LIMIT = 40 * 1024 * 1024
+WHOLE = 62 * 1024 * 1024
 
 
 def dot(left, right):
@@ -37,9 +38,9 @@
     return values * lax.rsqrt(jnp.mean(values * values, axis=-1, keepdims=True) + EPSILON)
 
 
-def pack_kernel(place_ref, tokens_ref, mix_ref, recur_ref, last_ref, packed_ref, *rest):
-    block_refs, (packed, blocks, sems, out_sems) = rest[:4], rest[4:]
-    c, x, h = place_ref[0], place_ref[1], place_ref[2]
+def pack_kernel(place_ref, tokens_ref, mix_ref, recur_ref, last_ref, *rest):
+    packed_refs, block_refs, (packed, blocks, sems, out_sems) = rest[:2], rest[2:6], rest[6:]
+    x, c, h = place_ref[0], place_ref[1], place_ref[2]
     copies = []
 
     def copy(source, through, target):
@@ -48,16 +49,19 @@
         copies.append((inward, pltpu.make_async_copy(through, target, out_sems.at[i])))
         inward.start()
 
-    def pack(source, rows):
-        copy(source, packed.at[rows, :], packed_ref.at[rows, :])
-
-    for q in range(2):
-        columns = pl.ds(pl.multiple_of(c * (2 * C) + q * C, C), C)
-        pack(mix_ref.at[:, columns], slice(q * C, (q + 1) * C))
-        pack(last_ref.at[:, columns], slice((8 + q) * C, (9 + q) * C))
-    for i in range(3):
-        half = pl.ds(pl.multiple_of(c * (D // 2), D // 2), D // 2)
-        pack(recur_ref.at[i, half, :], slice((i + 1) * D // 2, (i + 2) * D // 2))
+    for i, packed_ref in enumerate(packed_refs):
+        part = c if i == 0 else 1 - c
+
+        def pack(source, rows):
+            copy(source, packed.at[i, rows, :], packed_ref.at[rows, :])
+
+        for q in range(2):
+            columns = pl.ds(pl.multiple_of(part * (2 * C) + q * C, C), C)
+            pack(mix_ref.at[:, columns], slice(q * C, (q + 1) * C))
+            pack(last_ref.at[:, columns], slice((8 + q) * C, (9 + q) * C))
+        for k in range(3):
+            half = pl.ds(pl.multiple_of(part * (D // 2), D // 2), D // 2)
+            pack(recur_ref.at[k, half, :], slice((k + 1) * D // 2, (k + 2) * D // 2))
     for s, block_ref in enumerate(block_refs):
         part = tokens_ref.at[:, lax.rem(x + s, 4), pl.ds(pl.multiple_of(h * STRIDE, 16), SHARE), :]
         copy(part, blocks.at[s], block_ref)
@@ -68,21 +72,33 @@
         outward.wait()
 
 
-def attend_kernel(x_ref, order_ref, decay_ref, clip_ref, weight_ref, out_ref, normed, qkv, arranged, mixed):
+def attend_kernel(f, x_ref, order_ref, decay_ref, clip_ref, weight_ref, *rest):
+    out_ref, held, weight, normed, qkv, arranged, mixed, sems = rest[-8:]
     step = 112
+
+    def token_copy(i):
+        rows = pl.ds(pl.multiple_of(i * step, 16), step)
+        return pltpu.make_async_copy(x_ref.at[f, rows, :], held.at[rows, :], sems.at[i])
+
+    weight_copy = pltpu.make_async_copy(weight_ref, weight, sems.at[TOK // step])
+    for i in range(TOK // step):
+        token_copy(i).start()
+    weight_copy.start()
 
     def norm_step(i, carry):
         rows = pl.ds(pl.multiple_of(i * step, 16), step)
-        normed[rows, :] = scaled(x_ref[0, rows, :].astype(F32)).astype(BF16)
+        token_copy(i).wait()
+        normed[rows, :] = scaled(held[rows, :].astype(F32)).astype(BF16)
         return carry
 
     lax.fori_loop(0, TOK // step, norm_step, 0)
 
+    weight_copy.wait()
     half = TOK // 2
     for i in range(2):
         for k in range(3):
             rows = slice(i * half, (i + 1) * half)
-            qkv[rows, k * C : (k + 1) * C] = dot(normed[rows, :], weight_ref[k]).astype(BF16)
+            qkv[rows, k * C : (k + 1) * C] = dot(normed[rows, :], weight[k]).astype(BF16)
 
     lanes = lax.broadcasted_iota(jnp.int32, (128, TOK), 1)
     columns = jnp.transpose(order_ref[0])
@@ -132,8 +148,7 @@
 
     lax.fori_loop(0, WINDOWS // group, window_step, 0)
 
-    f = pl.program_id(0)
-    decay = decay_ref[pl.ds(f, 1), :]
+    decay = decay_ref[f : f + 1, :]
     clip = clip_ref[f].astype(F32)
     high = decay.astype(BF16).astype(F32)
     middle = (decay - high).astype(BF16).astype(F32)
@@ -161,51 +176,79 @@
     lax.fori_loop(0, 4, restore_step, 0)
 
 
-def attend(tokens, window_order, frame_decay, clip_id, weight):
-    padded = jnp.pad(
+def in_windows(window_order):
+    return jnp.pad(
         window_order.reshape(FRAMES, WINDOWS, WINDOW),
         ((0, 0), (0, 0), (0, SLOT - WINDOW)),
         constant_values=-1,
     ).reshape(FRAMES, ROWS // 128, 128)
+
+
+def attend(f, tokens, order, frame_decay, clip_id, weight, *held):
+    fixed = lambda shape, at: pl.BlockSpec(shape, lambda n: at, pipeline_mode=pl.Buffered(1))
     return pl.pallas_call(
-        attend_kernel,
-        grid=(FRAMES,),
+        functools.partial(attend_kernel, f),
+        grid=(1,),
         in_specs=[
-            pl.BlockSpec((1, TOK, D), lambda f: (f, 0, 0)),
-            pl.BlockSpec((1, ROWS // 128, 128), lambda f: (f, 0, 0)),
-            pl.BlockSpec((FRAMES, C), lambda f: (0, 0)),
+            pl.BlockSpec(memory_space=pltpu.HBM),
+            fixed((1, ROWS // 128, 128), (f, 0, 0)),
+            fixed((FRAMES, C), (0, 0)),
             pl.BlockSpec(memory_space=pltpu.SMEM),
-            pl.BlockSpec((3, D, C), lambda f: (0, 0, 0), pipeline_mode=pl.Buffered(1)),
-        ],
-        out_specs=pl.BlockSpec((16, 1, SENT, C), lambda f: (0, f, 0, 0)),
+            pl.BlockSpec(memory_space=pltpu.HBM),
+        ]
+        + [pl.BlockSpec(memory_space=pltpu.HBM)] * len(held),
+        out_specs=fixed((16, 1, SENT, C), (0, f, 0, 0)),
         out_shape=jax.ShapeDtypeStruct((16, FRAMES, SENT, C), BF16),
         scratch_shapes=[
+            pltpu.VMEM((TOK, D), BF16),
+            pltpu.VMEM((3, D, C), BF16),
             pltpu.VMEM((TOK, D), BF16),
             pltpu.VMEM((TOK, 3 * C), BF16),
             pltpu.VMEM((ROWS, 3 * C), BF16),
             pltpu.VMEM((ROWS, C), BF16),
-        ],
-        compiler_params=pltpu.CompilerParams(vmem_limit_bytes=LIMIT),
+            pltpu.SemaphoreType.DMA((15,)),
+        ],
+        input_output_aliases={5: 0} if held else {},
+        compiler_params=pltpu.CompilerParams(vmem_limit_bytes=WHOLE),
         cost_estimate=pl.CostEstimate(
-            flops=2 * FRAMES * (TOK * D * 3 * C + ROWS * TOK * 3 * C + 4 * ROWS * C * C + ROWS * TOK * C),
-            bytes_accessed=FRAMES * TOK * D * 4,
-            transcendentals=FRAMES * ROWS * C,
+            flops=2 * (TOK * D * 3 * C + ROWS * TOK * 3 * C + 4 * ROWS * C * C + ROWS * TOK * C),
+            bytes_accessed=TOK * D * 4,
+            transcendentals=ROWS * C,
         ),
         name="attend",
-    )(tokens, padded, frame_decay, clip_id, weight)
+    )(tokens, order, frame_decay, clip_id, weight, *held)
+
+
+def weight_copies(place_ref, weight_refs, held, sems, first, rows):
+    c, h = place_ref[1], place_ref[2]
+    near, far = lax.rem(h + 3 + 2 * c, 4), lax.rem(h + 1 + 2 * c, 4)
+    places = [(c, h), (1 - c, h), (c, near), (1 - c, near), (1 - c, far), (c, far)]
+    places += [(c, lax.rem(h + 2, 4)), (1 - c, lax.rem(h + 2, 4))]
+    return [
+        pltpu.make_async_copy(
+            weight_ref.at[first : first + rows, :], held.at[half, index, first : first + rows, :], sems.at[i]
+        )
+        for i, (weight_ref, (half, index)) in enumerate(zip(weight_refs, places))
+    ]
 
 
 def recur_kernel(
-    place_ref, att_ref, x0_ref, x1_ref, x2_ref, x3_ref, mix_ref, gate_ref, value_ref, open_ref,
-    residual_ref, state_ref, decay_ref, open_out_ref, last_ref,
-    normed,
+    place_ref, att_ref, x0_ref, x1_ref, x2_ref, x3_ref, *rest
 ):
+    weight_refs = rest[:8]
+    residual_ref, state_ref, decay_ref, open_out_ref, last_ref, normed, held, sems = rest[8:]
     x = place_ref[0]
     h = pl.program_id(0)
     count = FRAMES * SHARE
 
     @pl.when(h == 0)
     def _():
+        mix_copies = weight_copies(place_ref, weight_refs, held, sems.at[0], 0, D // 2)
+        recur_copies = weight_copies(place_ref, weight_refs, held, sems.at[1], D // 2, 3 * D // 2)
+        for one in mix_copies + recur_copies:
+            one.start()
+        for one in mix_copies:
+            one.wait()
         for s, x_ref in enumerate((x0_ref, x1_ref, x2_ref, x3_ref)):
             source = lax.rem(x + (4 - s), 4)
             pieces = []
@@ -214,20 +257,23 @@
                     total = None
                     for k in range(4):
                         left = att_ref[4 * source + k, :, :SHARE, :].reshape(count, C)
-                        term = dot(left, mix_ref[c, k, q * C : (q + 1) * C, :])
+                        term = dot(left, held[c, k, q * C : (q + 1) * C, :])
                         total = term if total is None else total + term
                     pieces.append(total)
             residual = x_ref[...].reshape(count, D).astype(F32) + jnp.concatenate(pieces, axis=1)
             residual_ref[source] = residual
             normed[source] = scaled(residual).astype(BF16)
+        for one in recur_copies:
+            one.wait()
 
     rows = normed[...].reshape(4 * count, D)
 
-    def project(ref):
-        return dot(rows[:, : D // 2], ref[0, 0]) + dot(rows[:, D // 2 :], ref[1, 0])
-
-    driven = jax.nn.sigmoid(project(gate_ref)) * project(value_ref)
-    opening = project(open_ref)
+    def project(i):
+        part = slice((i + 1) * D // 2, (i + 2) * D // 2)
+        return dot(rows[:, : D // 2], held[0, h, part, :]) + dot(rows[:, D // 2 :], held[1, h, part, :])
+
+    driven = jax.nn.sigmoid(project(0)) * project(1)
+    opening = project(2)
     open_out_ref[0] = opening * jax.nn.sigmoid(opening)
     state = jnp.zeros((SHARE, C), F32)
     first = before = None
@@ -249,11 +295,16 @@
     decay_ref[0, 8:, :] = jnp.broadcast_to(first, (8, C))
 
 
-def finish_kernel(state_ref, decay_ref, open_ref, incoming_ref, residual_ref, weight_ref, out_ref, rows):
+def finish_kernel(place_ref, state_ref, decay_ref, open_ref, incoming_ref, residual_ref, *rest):
+    weight_refs = rest[:8]
+    out_ref, rows, held, sems = rest[8:]
     n = pl.program_id(0)
 
     @pl.when(n == 0)
     def _():
+        copies = weight_copies(place_ref, weight_refs, held, sems, 2 * D, D // 2)
+        for one in copies:
+            one.start()
         for k in range(4):
             continues = incoming_ref[k, SHARE:, :].astype(F32) == decay_ref[k, 8:, :]
             incoming = incoming_ref[k, :SHARE, :].astype(F32) * jnp.where(continues, 1.0, 0.0)[:1]
@@ -261,10 +312,13 @@
                 piece = slice(f * SHARE, (f + 1) * SHARE)
                 state = state_ref[k, piece, :] + decay_ref[k, f : f + 1, :] * incoming
                 rows[k, piece, :] = (state * open_ref[k, piece, :]).astype(BF16)
+        for one in copies:
+            one.wait()
 
     total = residual_ref[...].reshape(8 * SHARE, C)
+    part = pl.ds(pl.multiple_of(2 * D + lax.rem(n, 2) * C, C), C)
     for k in range(4):
-        total = total + dot(rows[k], weight_ref[0, k])
+        total = total + dot(rows[k], held[n // 2, k, part, :])
     out_ref[...] = total.reshape(4, 1, FRAMES, SHARE, C).astype(BF16)
 
 
@@ -289,32 +343,54 @@
 def per_device(tokens, window_order, clip_id, attend_weight, attend_out, recur_weight, frame_decay, recur_out):
     c, z, x, h = (lax.axis_index(name) for name in ("clip", "z", "x", "head"))
 
-    here = pl.BlockSpec(memory_space=pl.ANY)
-    packed, *blocks = pl.pallas_call(
+    place = jnp.stack([x, c, h])
+    here = pl.BlockSpec(memory_space=pltpu.HBM)
+    first, second, *blocks = pl.pallas_call(
         pack_kernel,
         in_specs=[pl.BlockSpec(memory_space=pltpu.SMEM), here, here, here, here],
-        out_specs=[here] * 5,
-        out_shape=[jax.ShapeDtypeStruct((5 * D // 2, C), BF16)]
+        out_specs=[here] * 6,
+        out_shape=[jax.ShapeDtypeStruct((5 * D // 2, C), BF16)] * 2
         + [jax.ShapeDtypeStruct((FRAMES, SHARE, D), BF16)] * 4,
         scratch_shapes=[
-            pltpu.VMEM((5 * D // 2, C), BF16),
+            pltpu.VMEM((2, 5 * D // 2, C), BF16),
             pltpu.VMEM((4, FRAMES, SHARE, D), BF16),
-            pltpu.SemaphoreType.DMA((11,)),
-            pltpu.SemaphoreType.DMA((11,)),
+            pltpu.SemaphoreType.DMA((18,)),
+            pltpu.SemaphoreType.DMA((18,)),
         ],
         name="pack",
-    )(jnp.stack([c, x, h]), tokens.reshape(FRAMES, 4, QUARTER, D), attend_out, recur_weight, recur_out)
-    weights = lax.all_gather(packed, ("clip", "head"), axis=0).reshape(2, 4, 5 * D // 2, C)
+    )(place, tokens.reshape(FRAMES, 4, QUARTER, D), attend_out, recur_weight, recur_out)
+    def pinned(value):
+        return pltpu.with_memory_space_constraint(value, pltpu.HBM)
+
+    def onward(value):
+        pairs = [(i, (i + 1) % 4) for i in range(4)] + [(4 + i, 4 + (i + 3) % 4) for i in range(4)]
+        return lax.ppermute(value, ("clip", "head"), pairs)
+
+    def across(value):
+        return lax.ppermute(value, "clip", [(0, 1), (1, 0)])
+
+    near_first = onward(first)
+    near_second = onward(second)
     moved = [
         lax.ppermute(blocks[s], "x", [(i, (i + s) % 4) for i in range(4)]) if s else blocks[0] for s in range(4)
     ]
 
-    mixed = attend(tokens, window_order, frame_decay, clip_id, attend_weight)
-    mixed, *moved = lax.optimization_barrier((mixed, *moved))
+    order = in_windows(window_order)
+    tokens, attend_weight = pinned(tokens), pinned(attend_weight)
+    mixed = attend(0, tokens, order, frame_decay, clip_id, attend_weight)
+    mixed, near_first = lax.optimization_barrier((mixed, near_first))
+    far_first = onward(near_first)
+    other_first = across(near_first)
+    mixed = attend(1, tokens, order, frame_decay, clip_id, attend_weight, mixed)
+    mixed, near_second, far_first, other_first, *moved = lax.optimization_barrier(
+        (mixed, near_second, far_first, other_first, *moved)
+    )
+    other_second = across(near_second)
+    far_second = across(far_first)
+    weights = (first, second, near_first, near_second, other_first, other_second, far_first, far_second)
     mixed = lax.all_to_all(mixed, ("x", "head"), 0, 0)
 
     whole = lambda shape: pl.BlockSpec(shape, lambda n: (0,) * len(shape), pipeline_mode=pl.Buffered(1))
-    span = D // 2
     wide = 8 * SHARE
     residual, state, decay, opened, last = pl.pallas_call(
         recur_kernel,
@@ -326,10 +402,7 @@
             whole((FRAMES, SHARE, D)),
             whole((FRAMES, SHARE, D)),
             whole((FRAMES, SHARE, D)),
-            pl.BlockSpec((2, 4, span, C), lambda n: (0, 0, 0, 0)),
-            pl.BlockSpec((2, 1, span, C), lambda n: (0, n, 1, 0)),
-            pl.BlockSpec((2, 1, span, C), lambda n: (0, n, 2, 0)),
-            pl.BlockSpec((2, 1, span, C), lambda n: (0, n, 3, 0)),
+            *[here] * 8,
         ],
         out_specs=[
             pl.BlockSpec((4, FRAMES * SHARE, D), lambda n: (0, 0, 0)),
@@ -345,10 +418,14 @@
             jax.ShapeDtypeStruct((4, wide, C), F32),
             jax.ShapeDtypeStruct((4, SENT, C), BF16),
         ],
-        scratch_shapes=[pltpu.VMEM((4, FRAMES * SHARE, D), BF16)],
+        scratch_shapes=[
+            pltpu.VMEM((4, FRAMES * SHARE, D), BF16),
+            pltpu.VMEM((2, 4, 2 * D, C), BF16),
+            pltpu.SemaphoreType.DMA((2, 8)),
+        ],
         compiler_params=pltpu.CompilerParams(vmem_limit_bytes=LIMIT),
         name="recur",
-    )(x[None], mixed, *moved, weights, weights, weights, weights)
+    )(place, mixed, *map(pinned, moved), *map(pinned, weights))
 
     incoming = lax.ppermute(last, "z", [(i, i + 1) for i in range(3)])
 
@@ -356,19 +433,24 @@
         finish_kernel,
         grid=(4,),
         in_specs=[
+            pl.BlockSpec(memory_space=pltpu.SMEM),
             whole((4, wide, C)),
             whole((4, 16, C)),
             whole((4, wide, C)),
             whole((4, SENT, C)),
             pl.BlockSpec((4, FRAMES * SHARE, C), lambda n: (0, 0, n)),
-            pl.BlockSpec((1, 4, C, C), lambda n: (n // 2, 0, 8 + n % 2, 0)),
+            *[here] * 8,
         ],
         out_specs=pl.BlockSpec((4, 1, FRAMES, SHARE, C), lambda n: (0, n, 0, 0, 0)),
         out_shape=jax.ShapeDtypeStruct((4, 4, FRAMES, SHARE, C), BF16),
-        scratch_shapes=[pltpu.VMEM((4, wide, C), BF16)],
+        scratch_shapes=[
+            pltpu.VMEM((4, wide, C), BF16),
+            pltpu.VMEM((2, 4, 5 * D // 2, C), BF16),
+            pltpu.SemaphoreType.DMA((8,)),
+        ],
         compiler_params=pltpu.CompilerParams(vmem_limit_bytes=LIMIT),
         name="finish",
-    )(state, decay, opened, incoming, residual, weights)
+    )(place, state, decay, opened, incoming, residual, *map(pinned, weights))
 
     result = lax.all_to_all(result.reshape(16, FRAMES, SHARE, C), ("x", "head"), 0, 0)
     placed = pl.pallas_call(

time: 155 us -> 143 us (0.923)
  blocking collectives: 62 us -> 25.9 us
  waiting for transfers between devices: 9.75 us -> 31.4 us
  between operations: 13.5 us -> 0.34 us
  starting transfers between devices: 9.2 us -> 18.5 us
  Pallas kernels: 56.8 us -> 64.6 us
  local copies, waits for them, and re-layouts: 3.02 us -> 0.8 us
    all_to_all x1 -> x0, blocking collectives: 32.7 us -> none  [per_device(): mixed = lax.all_to_all(mixed, ('x', 'head'), 0, 0)]
    all_to_all x0 -> x1, waiting for transfers between devices: none -> 22.6 us  [per_device(): mixed = lax.all_to_all(mixed, ('x', 'head'), 0, 0)]
    pallas_call x2 -> x3, Pallas kernels: 40.1 us -> 45.4 us  [the longest x2 40.4 us: attend(): pl.pallas_call(functools.partial(attend_kernel, f), grid=(1,), in_specs=[...]
    ppermute x0 -> x6, starting transfers between devices: none -> 5.24 us  [the longest x3 4.57 us: onward(): return lax.ppermute(value, ('clip', 'head'), pairs)]
    ppermute x0 -> x6, waiting for transfers between devices: none -> 4.75 us  [the longest x3 4.74 us: across(): return lax.ppermute(value, 'clip', [(0, 1), (1, 0)])]
    all_to_all x0 -> x1, starting transfers between devices: none -> 3.72 us  [per_device(): mixed = lax.all_to_all(mixed, ('x', 'head'), 0, 0)]
    all_gather x1 -> x0, waiting for transfers between devices: 3.54 us -> none  [per_device(): lax.all_gather(packed, ('clip', 'head'), axis=0)]
    all_to_all x1, blocking collectives: 29.3 us -> 25.9 us  [per_device(): lax.all_to_all(result.reshape(16, FRAMES, SHARE, C), ('x', 'head'), 0, 0)]
  transfers between devices with their start and end apart: 5 -> 11, of which waited for: 2 -> 4; matrix products, arithmetic and copies ran while one was open for 0% -> 1% of each run, Pallas kernels for 23% -> 28%
where the time goes in v3:
time: 143 us; the launch traced here: 142 us
  Pallas kernels  64.6 us (45%)
  waiting for transfers between devices  31.4 us (22%)
  blocking collectives  25.9 us (18%)
  starting transfers between devices  18.5 us (13%)
    pallas_call x2, Pallas kernels, attend(): pl.pallas_call(functools.partial(attend_kernel, f), grid=(1,), in_specs=[...  40.4 us
    all_to_all x1, blocking collectives, per_device(): lax.all_to_all(result.reshape(16, FRAMES, SHARE, C), ('x', 'head'), 0, 0)  25.9 us
    all_to_all x1, waiting for transfers between devices, per_device(): mixed = lax.all_to_all(mixed, ('x', 'head'), 0, 0)  22.6 us
    pallas_call x1, Pallas kernels, per_device(): pl.pallas_call(recur_kernel, grid=(4,), in_specs=[pl.BlockSpec(memory_spa...  11.5 us
    ppermute x3, starting transfers between devices, per_device(): lax.ppermute(blocks[s], 'x', [(i, (i + s) % 4) for i in range(4)])  5.65 us
    pallas_call x1, Pallas kernels, per_device(): pl.pallas_call(pack_kernel, in_specs=[pl.BlockSpec(memory_space=pltpu.SME...  5.3 us
    pallas_call x1, Pallas kernels, per_device(): pl.pallas_call(finish_kernel, grid=(4,), in_specs=[pl.BlockSpec(memory_sp...  5.03 us
    ppermute x3, waiting for transfers between devices, across(): return lax.ppermute(value, 'clip', [(0, 1), (1, 0)])  4.74 us
  transfers between devices with their start and end apart: 11, of which 4 were waited for; matrix products, arithmetic and copies ran while one was open for 1% of the time, Pallas kernels for 28%

profile of v3, /device:TPU:32, one launch (start us, length us, event | category | flops | bytes accessed | tf_op | source)
XLA Modules:
  0.0 142.1 jit_solution(1746639764901712316)
XLA Ops:
  0.0 0.6 pad_add_fusion.place_ref
  0.6 5.3 %pack.1 = (bf16[2560,256]{1,0:T(8,128)(2,1)}, bf16[2560,256]{1,0:T(8,128)(2,1)}, bf16[2,104,1024]{2,1,0:T(8,128)(2,1)}, bf16[2,104,1024]{2,1,0:T(8,128)(2,1)}, b...) custom-call(s32[3]{0:T(128)} %pad_add_fusion.place_ref, bf16[2,4,392,1024]{3,2,1,0:T(8,128)(2,1)} %bitcast.9, ...), custom_call_target="tpu_custom_call" | custom-call | tf_op jit(solution)/shard_map/pack/pallas_call | solution.py:348
  5.9 1.6 %collective-permute-start = (bf16[2560,256]{1,0:T(8,128)(2,1)}, bf16[2560,256]{1,0:T(8,128)(2,1)S(1)}, u32[]{:S(2)}, u32[]{:S(2)}) collective-permute-start(bf16[2560,256]{1,0:T(8,128)(2,1)} %get-tuple-element.26.rest_0_), channel_id=1, source_target_pairs={{0,1},{1,2},{2,3},{3,0},{64,67},{65,64},{66,65},{67,66},{4,5},{5,6... | collective-permute-start | bytes 3932168 | tf_op jit(solution)/shard_map/ppermute | solution.py:367
  7.6 1.5 %collective-permute-start.4 = (bf16[2,104,1024]{2,1,0:T(8,128)(2,1)}, bf16[2,104,1024]{2,1,0:T(8,128)(2,1)S(1)}, u32[]{:S(2)}, u32[]{:S(2)}) collective-permute-start(bf16[2,104,1024]{2,1,0:T(8,128)(2,1)} %get-tuple-element.31), channel_id=1, source_target_pairs={{0,4},{4,8},{8,12},{12,0},{1,5},{5,9},{9,13},{13,1},{2,6},{6,10},{... | collective-permute-start | bytes 1277960 | tf_op jit(solution)/shard_map/ppermute | solution.py:375
  9.1 1.6 %collective-permute-start.1 = (bf16[2560,256]{1,0:T(8,128)(2,1)}, bf16[2560,256]{1,0:T(8,128)(2,1)}, u32[]{:S(2)}, u32[]{:S(2)}) collective-permute-start(bf16[2560,256]{1,0:T(8,128)(2,1)} %get-tuple-element.28.rest_1_), channel_id=1, source_target_pairs={{0,1},{1,2},{2,3},{3,0},{64,67},{65,64},{66,65},{67,66},{4,5},{5,6... | collective-permute-start | bytes 3932168 | tf_op jit(solution)/shard_map/ppermute | solution.py:367
  10.6 0.1 reshape.18
  10.8 0.7 reshape.19.order_ref
  11.4 20.2 %attend.2.rest_0_ = bf16[16,2,112,256]{3,2,1,0:T(8,128)(2,1)} custom-call(bf16[2,1568,1024]{2,1,0:T(8,128)(2,1)} %x_ref.3, s32[2,16,128]{2,1,0:T(8,128)} %reshape.19.order_ref, f32[2,256]{1,0:T(2,128)} %decay_ref.3, s32[2]{0:T(128)} %clip_ref.3, bf16[3,1024,256]{2,1,0:T(8,128)(2,1)} %weight_ref.3), custom_call_target="tpu_custom_call" | custom-call | flops 10116661248 | bytes 6422528 | tf_op jit(solution)/shard_map/attend/pallas_call | solution.py:189
  31.6 0.0 collective-permute-done.rest_2_
  31.6 0.1 collective-permute-start.3
  31.7 1.4 collective-permute-start.2
  33.1 2.7 %collective-permute-start.5 = (bf16[2,104,1024]{2,1,0:T(8,128)(2,1)}, bf16[2,104,1024]{2,1,0:T(8,128)(2,1)}, u32[]{:S(2)}, u32[]{:S(2)}) collective-permute-start(bf16[2,104,1024]{2,1,0:T(8,128)(2,1)} %get-tuple-element.32), channel_id=1, source_target_pairs={{0,8},{4,12},{8,0},{12,4},{1,9},{5,13},{9,1},{13,5},{2,10},{6,14},... | collective-permute-start | bytes 1277960 | tf_op jit(solution)/shard_map/ppermute | solution.py:375
  35.8 0.0 collective-permute-done.4.x1_ref
  35.8 1.4 %collective-permute-start.6 = (bf16[2,104,1024]{2,1,0:T(8,128)(2,1)}, bf16[2,104,1024]{2,1,0:T(8,128)(2,1)}, u32[]{:S(2)}, u32[]{:S(2)}) collective-permute-start(bf16[2,104,1024]{2,1,0:T(8,128)(2,1)} %get-tuple-element.33), channel_id=1, source_target_pairs={{0,12},{4,0},{8,4},{12,8},{1,13},{5,1},{9,5},{13,9},{2,14},{6,2},{... | collective-permute-start | bytes 1277960 | tf_op jit(solution)/shard_map/ppermute | solution.py:375
  37.3 20.2 %attend.3 = bf16[16,2,112,256]{3,2,1,0:T(8,128)(2,1)} custom-call(bf16[2,1568,1024]{2,1,0:T(8,128)(2,1)} %x_ref.3, s32[2,16,128]{2,1,0:T(8,128)} %reshape.19.order_ref, f32[2,256]{1,0:T(2,128)} %decay_ref.3, s32[2]{0:T(128)} %clip_ref.3, bf16[3,1024,256]{2,1,0:T(8,128)(2,1)} %weight_ref.3, ...), custom_call_target="tpu_custom_call", output_to_operand_aliasing={{}: (5, {})} | custom-call | flops 10116661248 | bytes 6422528 | tf_op jit(solution)/shard_map/attend/pallas_call | solution.py:189
  57.5 0.0 collective-permute-done.5.x2_ref
  57.5 0.0 collective-permute-done.6.x3_ref
  57.5 0.0 collective-permute-done.1.rest_3_
  57.5 0.0 collective-permute-done.3.rest_4_
  57.5 0.0 collective-permute-done.2.rest_6_
  57.5 3.7 %all-to-all-start = ((bf16[16,2,112,256]{3,2,1,0:T(8,128)(2,1)}), bf16[16,2,112,256]{3,2,1,0:T(8,128)(2,1)S(1)}, u32[]{:S(2)}, u32[]{:S(2)}) async-start(bf16[16,2,112,256]{3,2,1,0:T(8,128)(2,1)} %attend.3), calls=%async_computation | async-start | bytes 3670016 | tf_op jit(solution)/shard_map/all_to_all | solution.py:391
  61.3 0.1 collective-permute-start.7
  61.4 0.5 collective-permute-start.8
  61.9 3.7 %collective-permute-done.7.rest_5_ = bf16[2560,256]{1,0:T(8,128)(2,1)S(1)} collective-permute-done((bf16[2560,256]{1,0:T(8,128)(2,1)}, bf16[2560,256]{1,0:T(8,128)(2,1)S(1)}, u32[]{:S(2)}, u32[]{:S(2)}) %collective-permute-start.7) | collective-permute-done | bytes 1310752 | tf_op jit(solution)/shard_map/ppermute | solution.py:370
  65.5 1.1 collective-permute-done.8.rest_7_
  66.6 22.6 %all-to-all-done.att_ref = bf16[16,2,112,256]{3,2,1,0:T(8,128)(2,1)S(1)} async-done(((bf16[16,2,112,256]{3,2,1,0:T(8,128)(2,1)}), bf16[16,2,112,256]{3,2,1,0:T(8,128)(2,1)S(1)}, u32[]{:S(2)}, u32[]{:S(2)}) %all-to-all-start) | async-done | bytes 1835040 | tf_op jit(solution)/shard_map/all_to_all | solution.py:391
  89.2 11.5 %recur.1 = (f32[4,208,1024]{2,1,0:T(8,128)S(1)}, f32[4,832,256]{2,1,0:T(8,128)S(1)}, f32[4,16,256]{2,1,0:T(8,128)S(1)}, f32[4,832,256]{2,1,0:T(8,128)S(1)}, bf16[4,112,256]{2,1,0:T(8,128)(2,1)S(1)}) custom-call(s32[3]{0:T(128)S(1)} %copy-done, bf16[16,2,112,256]{3,2,1,0:T(8,128)(2,1)S(1)} %all-to-all-done.att_ref, ...), custom_call_target="tpu_custom_call" | custom-call | tf_op jit(solution)/shard_map/recur/pallas_call | solution.py:395
  100.6 3.8 %collective-permute-start.9 = (bf16[4,112,256]{2,1,0:T(8,128)(2,1)S(1)}, bf16[4,112,256]{2,1,0:T(8,128)(2,1)S(1)}, u32[]{:S(2)}, u32[]{:S(2)}) collective-permute-start(bf16[4,112,256]{2,1,0:T(8,128)(2,1)S(1)} %get-tuple-element.45), channel_id=1, source_target_pairs={{0,16},{16,32},{32,48},{1,17},{17,33},{33,49},{2,18},{18,34},{34,5... | collective-permute-start | bytes 688136 | tf_op jit(solution)/shard_map/ppermute | solution.py:430
  104.5 4.1 %collective-permute-done.9.incoming_ref = bf16[4,112,256]{2,1,0:T(8,128)(2,1)S(1)} collective-permute-done((bf16[4,112,256]{2,1,0:T(8,128)(2,1)S(1)}, bf16[4,112,256]{2,1,0:T(8,128)(2,1)S(1)}, u32[]{:S(2)}, u32[]{:S(2)}) %collective-permute-start.9) | collective-permute-done | bytes 229408 | tf_op jit(solution)/shard_map/ppermute | solution.py:430
  108.5 5.0 %finish.1 = bf16[4,4,2,104,256]{4,3,2,1,0:T(8,128)(2,1)S(1)} custom-call(s32[3]{0:T(128)S(1)} %copy-done, f32[4,832,256]{2,1,0:T(8,128)S(1)} %get-tuple-element.42.state_ref, f32[4,16,256]{2,1,0:T(8,128)S(1)} %get-tuple-element.43.decay_ref, f32[4,832,256]{2,1,0:T(8,128)S(1)} %get-tuple-element.44.open_ref, ...), custom_call_target="tpu_custom_call" | custom-call | tf_op jit(solution)/shard_map/finish/pallas_call | solution.py:432
  113.6 25.9 %all_to_all.10 = bf16[16,2,104,256]{3,2,1,0:T(8,128)(2,1)} all-to-all(bf16[16,2,104,256]{3,2,1,0:T(8,128)(2,1)S(1)} %bitcast.7), channel_id=1, replica_groups=mesh['clip'=2,'z'=4,'x'=4,'head'=4] {'x','head'}, dimensions={0} | all-to-all | bytes 3407872 | tf_op jit(solution)/shard_map/all_to_all | solution.py:455
  139.5 2.4 %place.1 = bf16[2,4,392,256]{3,2,1,0:T(8,128)(2,1)} custom-call(bf16[4,4,2,104,256]{4,3,2,1,0:T(8,128)(2,1)} %bitcast.8), custom_call_target="tpu_custom_call" | custom-call | tf_op jit(solution)/shard_map/place/pallas_call | solution.py:456
  (11 shorter events, 0.0 us)
Async XLA Ops:
  0.6 10.0 %copy-start.4 = (s32[2,1568]{1,0:T(2,128)S(1)}, s32[2,1568]{1,0:T(2,128)}, u32[]{:S(2)}) copy-start(s32[2,1568]{1,0:T(2,128)} %param.9) | copy-start | bytes 37636
  5.9 25.7 %collective-permute-start = (bf16[2560,256]{1,0:T(8,128)(2,1)}, bf16[2560,256]{1,0:T(8,128)(2,1)S(1)}, u32[]{:S(2)}, u32[]{:S(2)}) collective-permute-start(bf16[2560,256]{1,0:T(8,128)(2,1)} %get-tuple-element.26.rest_0_), channel_id=1, source_target_pairs={{0,1},{1,2},{2,3},{3,0},{64,67},{65,64},{66,65},{67,66},{4,5},{5,6... | collective-permute-start | bytes 3932168 | tf_op jit(solution)/shard_map/ppermute | solution.py:367
  7.6 28.3 %collective-permute-start.4 = (bf16[2,104,1024]{2,1,0:T(8,128)(2,1)}, bf16[2,104,1024]{2,1,0:T(8,128)(2,1)S(1)}, u32[]{:S(2)}, u32[]{:S(2)}) collective-permute-start(bf16[2,104,1024]{2,1,0:T(8,128)(2,1)} %get-tuple-element.31), channel_id=1, source_target_pairs={{0,4},{4,8},{8,12},{12,0},{1,5},{5,9},{9,13},{13,1},{2,6},{6,10},{... | collective-permute-start | bytes 1277960 | tf_op jit(solution)/shard_map/ppermute | solution.py:375
  9.1 48.4 %collective-permute-start.1 = (bf16[2560,256]{1,0:T(8,128)(2,1)}, bf16[2560,256]{1,0:T(8,128)(2,1)}, u32[]{:S(2)}, u32[]{:S(2)}) collective-permute-start(bf16[2560,256]{1,0:T(8,128)(2,1)} %get-tuple-element.28.rest_1_), channel_id=1, source_target_pairs={{0,1},{1,2},{2,3},{3,0},{64,67},{65,64},{66,65},{67,66},{4,5},{5,6... | collective-permute-start | bytes 3932168 | tf_op jit(solution)/shard_map/ppermute | solution.py:367
  31.6 25.8 %copy-start.1 = (bf16[2560,256]{1,0:T(8,128)(2,1)}, bf16[2560,256]{1,0:T(8,128)(2,1)S(1)}, u32[]{:S(2)}) copy-start(bf16[2560,256]{1,0:T(8,128)(2,1)S(1)} %collective-permute-done.rest_2_) | copy-start | bytes 3932164
  31.6 25.9 %collective-permute-start.3 = (bf16[2560,256]{1,0:T(8,128)(2,1)S(1)}, bf16[2560,256]{1,0:T(8,128)(2,1)}, u32[]{:S(2)}, u32[]{:S(2)}) collective-permute-start(bf16[2560,256]{1,0:T(8,128)(2,1)S(1)} %collective-permute-done.rest_2_), channel_id=1, source_target_pairs={{0,64},{64,0},{1,65},{65,1},{2,66},{66,2},{3,67},{67,3},{4,68},{68... | collective-permute-start | bytes 3932168 | tf_op jit(solution)/shard_map/ppermute | solution.py:370
  31.7 25.8 %collective-permute-start.2 = (bf16[2560,256]{1,0:T(8,128)(2,1)S(1)}, bf16[2560,256]{1,0:T(8,128)(2,1)}, u32[]{:S(2)}, u32[]{:S(2)}) collective-permute-start(bf16[2560,256]{1,0:T(8,128)(2,1)S(1)} %collective-permute-done.rest_2_), channel_id=1, source_target_pairs={{0,1},{1,2},{2,3},{3,0},{64,67},{65,64},{66,65},{67,66},{4,5},{5,6... | collective-permute-start | bytes 3932168 | tf_op jit(solution)/shard_map/ppermute | solution.py:367
  33.1 24.4 %collective-permute-start.5 = (bf16[2,104,1024]{2,1,0:T(8,128)(2,1)}, bf16[2,104,1024]{2,1,0:T(8,128)(2,1)}, u32[]{:S(2)}, u32[]{:S(2)}) collective-permute-start(bf16[2,104,1024]{2,1,0:T(8,128)(2,1)} %get-tuple-element.32), channel_id=1, source_target_pairs={{0,8},{4,12},{8,0},{12,4},{1,9},{5,13},{9,1},{13,5},{2,10},{6,14},... | collective-permute-start | bytes 1277960 | tf_op jit(solution)/shard_map/ppermute | solution.py:375
  35.8 21.6 %copy-start.3 = (bf16[2,104,1024]{2,1,0:T(8,128)(2,1)}, bf16[2,104,1024]{2,1,0:T(8,128)(2,1)S(1)}, u32[]{:S(2)}) copy-start(bf16[2,104,1024]{2,1,0:T(8,128)(2,1)S(1)} %collective-permute-done.4.x1_ref) | copy-start | bytes 1277956
  35.8 21.6 %collective-permute-start.6 = (bf16[2,104,1024]{2,1,0:T(8,128)(2,1)}, bf16[2,104,1024]{2,1,0:T(8,128)(2,1)}, u32[]{:S(2)}, u32[]{:S(2)}) collective-permute-start(bf16[2,104,1024]{2,1,0:T(8,128)(2,1)} %get-tuple-element.33), channel_id=1, source_target_pairs={{0,12},{4,0},{8,4},{12,8},{1,13},{5,1},{9,5},{13,9},{2,14},{6,2},{... | collective-permute-start | bytes 1277960 | tf_op jit(solution)/shard_map/ppermute | solution.py:375
  57.5 31.6 %copy-start = (s32[3]{0:T(128)S(1)}, s32[3]{0:T(128)}, u32[]{:S(2)}) copy-start(s32[3]{0:T(128)} %pad_add_fusion.place_ref) | copy-start | bytes 40
  57.5 31.6 %all-to-all-start = ((bf16[16,2,112,256]{3,2,1,0:T(8,128)(2,1)}), bf16[16,2,112,256]{3,2,1,0:T(8,128)(2,1)S(1)}, u32[]{:S(2)}, u32[]{:S(2)}) async-start(bf16[16,2,112,256]{3,2,1,0:T(8,128)(2,1)} %attend.3), calls=%async_computation | async-start | bytes 3670016 | tf_op jit(solution)/shard_map/all_to_all | solution.py:391
  61.3 4.3 %collective-permute-start.7 = (bf16[2560,256]{1,0:T(8,128)(2,1)}, bf16[2560,256]{1,0:T(8,128)(2,1)S(1)}, u32[]{:S(2)}, u32[]{:S(2)}) collective-permute-start(bf16[2560,256]{1,0:T(8,128)(2,1)} %collective-permute-done.1.rest_3_), channel_id=1, source_target_pairs={{0,64},{64,0},{1,65},{65,1},{2,66},{66,2},{3,67},{67,3},{4,68},{68... | collective-permute-start | bytes 3932168 | tf_op jit(solution)/shard_map/ppermute | solution.py:370
  61.4 5.2 %collective-permute-start.8 = (bf16[2560,256]{1,0:T(8,128)(2,1)}, bf16[2560,256]{1,0:T(8,128)(2,1)}, u32[]{:S(2)}, u32[]{:S(2)}) collective-permute-start(bf16[2560,256]{1,0:T(8,128)(2,1)} %collective-permute-done.2.rest_6_), channel_id=1, source_target_pairs={{0,64},{64,0},{1,65},{65,1},{2,66},{66,2},{3,67},{67,3},{4,68},{68... | collective-permute-start | bytes 3932168 | tf_op jit(solution)/shard_map/ppermute | solution.py:370
  65.5 23.6 %copy-start.2 = (bf16[2560,256]{1,0:T(8,128)(2,1)}, bf16[2560,256]{1,0:T(8,128)(2,1)S(1)}, u32[]{:S(2)}) copy-start(bf16[2560,256]{1,0:T(8,128)(2,1)S(1)} %collective-permute-done.7.rest_5_) | copy-start | bytes 3932164
  100.6 7.9 %collective-permute-start.9 = (bf16[4,112,256]{2,1,0:T(8,128)(2,1)S(1)}, bf16[4,112,256]{2,1,0:T(8,128)(2,1)S(1)}, u32[]{:S(2)}, u32[]{:S(2)}) collective-permute-start(bf16[4,112,256]{2,1,0:T(8,128)(2,1)S(1)} %get-tuple-element.45), channel_id=1, source_target_pairs={{0,16},{16,32},{32,48},{1,17},{17,33},{33,49},{2,18},{18,34},{34,5... | collective-permute-start | bytes 688136 | tf_op jit(solution)/shard_map/ppermute | solution.py:430

commit v4 on v3

--- a/solution.py
+++ b/solution.py
@@ -74,7 +74,7 @@
 
 def attend_kernel(f, x_ref, order_ref, decay_ref, clip_ref, weight_ref, *rest):
     out_ref, held, weight, normed, qkv, arranged, mixed, sems = rest[-8:]
-    step = 112
+    step = 224
 
     def token_copy(i):
         rows = pl.ds(pl.multiple_of(i * step, 16), step)
@@ -114,7 +114,7 @@
     row_index = lax.broadcasted_iota(jnp.int32, (C, C), 0)
     lane_index = lax.broadcasted_iota(jnp.int32, (C, C), 1)
     together = jnp.where(row_index // HEAD == lane_index // HEAD, 1.0, 0.0).astype(BF16)
-    group = 4
+    group = 16
     lane = lax.broadcasted_iota(jnp.int32, (group * SLOT, 128), 1)
     low = lane < SLOT
     valid = (lane % SLOT) < WINDOW
@@ -173,7 +173,7 @@
             out_ref[4 * i + h, 0, SHARE:, :] = extra
         return carry
 
-    lax.fori_loop(0, 4, restore_step, 0)
+    lax.fori_loop(0, 4, restore_step, 0, unroll=4)
 
 
 def in_windows(window_order):
@@ -378,13 +378,11 @@
     order = in_windows(window_order)
     tokens, attend_weight = pinned(tokens), pinned(attend_weight)
     mixed = attend(0, tokens, order, frame_decay, clip_id, attend_weight)
-    mixed, near_first = lax.optimization_barrier((mixed, near_first))
+    mixed, near_first, moved[1], moved[3] = lax.optimization_barrier((mixed, near_first, moved[1], moved[3]))
     far_first = onward(near_first)
     other_first = across(near_first)
     mixed = attend(1, tokens, order, frame_decay, clip_id, attend_weight, mixed)
-    mixed, near_second, far_first, other_first, *moved = lax.optimization_barrier(
-        (mixed, near_second, far_first, other_first, *moved)
-    )
+    mixed, near_second, other_first, *moved = lax.optimization_barrier((mixed, near_second, other_first, *moved))
     other_second = across(near_second)
     far_second = across(far_first)
     weights = (first, second, near_first, near_second, other_first, other_second, far_first, far_second)

time: 143 us -> 135 us (0.944)
  Pallas kernels: 64.6 us -> 58.3 us
    pallas_call x2, Pallas kernels: 40.4 us -> 34.1 us  [attend(): pl.pallas_call(functools.partial(attend_kernel, f), grid=(1,), in_specs=[...]
  transfers between devices with their start and end apart: 11 -> 11, of which waited for: 4 -> 4; matrix products, arithmetic and copies ran while one was open for 1% -> 1% of each run, Pallas kernels for 28% -> 25%
where the time goes in v4:
time: 135 us; the launch traced here: 134 us
  Pallas kernels  58.3 us (43%)
  waiting for transfers between devices  30.9 us (23%)
  blocking collectives  24.6 us (18%)
  starting transfers between devices  18.6 us (14%)
    pallas_call x2, Pallas kernels, attend(): pl.pallas_call(functools.partial(attend_kernel, f), grid=(1,), in_specs=[...  34.1 us
    all_to_all x1, blocking collectives, per_device(): lax.all_to_all(result.reshape(16, FRAMES, SHARE, C), ('x', 'head'), 0, 0)  24.6 us
    all_to_all x1, waiting for transfers between devices, per_device(): mixed = lax.all_to_all(mixed, ('x', 'head'), 0, 0)  22 us
    pallas_call x1, Pallas kernels, per_device(): pl.pallas_call(recur_kernel, grid=(4,), in_specs=[pl.BlockSpec(memory_spa...  11.4 us
    pallas_call x1, Pallas kernels, per_device(): pl.pallas_call(pack_kernel, in_specs=[pl.BlockSpec(memory_space=pltpu.SME...  5.27 us
    ppermute x3, starting transfers between devices, per_device(): lax.ppermute(blocks[s], 'x', [(i, (i + s) % 4) for i in range(4)])  5.12 us
    pallas_call x1, Pallas kernels, per_device(): pl.pallas_call(finish_kernel, grid=(4,), in_specs=[pl.BlockSpec(memory_sp...  5.03 us
    ppermute x3, waiting for transfers between devices, across(): return lax.ppermute(value, 'clip', [(0, 1), (1, 0)])  4.74 us
  transfers between devices with their start and end apart: 11, of which 4 were waited for; matrix products, arithmetic and copies ran while one was open for 1% of the time, Pallas kernels for 25%

profile of v4, /device:TPU:32, one launch (start us, length us, event | category | flops | bytes accessed | tf_op | source)
XLA Modules:
  0.0 134.0 jit_solution(4783545661705907038)
XLA Ops:
  0.0 0.6 pad_add_fusion.place_ref
  0.6 5.3 %pack.1 = (bf16[2560,256]{1,0:T(8,128)(2,1)}, bf16[2560,256]{1,0:T(8,128)(2,1)}, bf16[2,104,1024]{2,1,0:T(8,128)(2,1)}, bf16[2,104,1024]{2,1,0:T(8,128)(2,1)}, b...) custom-call(s32[3]{0:T(128)} %pad_add_fusion.place_ref, bf16[2,4,392,1024]{3,2,1,0:T(8,128)(2,1)} %bitcast.9, ...), custom_call_target="tpu_custom_call" | custom-call | tf_op jit(solution)/shard_map/pack/pallas_call | solution.py:348
  5.9 1.6 %collective-permute-start = (bf16[2560,256]{1,0:T(8,128)(2,1)}, bf16[2560,256]{1,0:T(8,128)(2,1)S(1)}, u32[]{:S(2)}, u32[]{:S(2)}) collective-permute-start(bf16[2560,256]{1,0:T(8,128)(2,1)} %get-tuple-element.27.rest_0_), channel_id=1, source_target_pairs={{0,1},{1,2},{2,3},{3,0},{64,67},{65,64},{66,65},{67,66},{4,5},{5,6... | collective-permute-start | bytes 3932168 | tf_op jit(solution)/shard_map/ppermute | solution.py:367
  7.5 1.5 %collective-permute-start.1 = (bf16[2,104,1024]{2,1,0:T(8,128)(2,1)}, bf16[2,104,1024]{2,1,0:T(8,128)(2,1)}, u32[]{:S(2)}, u32[]{:S(2)}) collective-permute-start(bf16[2,104,1024]{2,1,0:T(8,128)(2,1)} %get-tuple-element.28), channel_id=1, source_target_pairs={{0,4},{4,8},{8,12},{12,0},{1,5},{5,9},{9,13},{13,1},{2,6},{6,10},{... | collective-permute-start | bytes 1277960 | tf_op jit(solution)/shard_map/ppermute | solution.py:375
  9.0 1.7 %collective-permute-start.2 = (bf16[2,104,1024]{2,1,0:T(8,128)(2,1)}, bf16[2,104,1024]{2,1,0:T(8,128)(2,1)}, u32[]{:S(2)}, u32[]{:S(2)}) collective-permute-start(bf16[2,104,1024]{2,1,0:T(8,128)(2,1)} %get-tuple-element.29), channel_id=1, source_target_pairs={{0,12},{4,0},{8,4},{12,8},{1,13},{5,1},{9,5},{13,9},{2,14},{6,2},{... | collective-permute-start | bytes 1277960 | tf_op jit(solution)/shard_map/ppermute | solution.py:375
  10.7 1.6 %collective-permute-start.3 = (bf16[2560,256]{1,0:T(8,128)(2,1)}, bf16[2560,256]{1,0:T(8,128)(2,1)}, u32[]{:S(2)}, u32[]{:S(2)}) collective-permute-start(bf16[2560,256]{1,0:T(8,128)(2,1)} %get-tuple-element.31.rest_1_), channel_id=1, source_target_pairs={{0,1},{1,2},{2,3},{3,0},{64,67},{65,64},{66,65},{67,66},{4,5},{5,6... | collective-permute-start | bytes 3932168 | tf_op jit(solution)/shard_map/ppermute | solution.py:367
  12.3 0.1 reshape.18
  12.5 0.7 reshape.19.order_ref
  13.1 17.1 %attend.2.rest_0_ = bf16[16,2,112,256]{3,2,1,0:T(8,128)(2,1)} custom-call(bf16[2,1568,1024]{2,1,0:T(8,128)(2,1)} %x_ref.3, s32[2,16,128]{2,1,0:T(8,128)} %reshape.19.order_ref, f32[2,256]{1,0:T(2,128)} %decay_ref.3, s32[2]{0:T(128)} %clip_ref.3, bf16[3,1024,256]{2,1,0:T(8,128)(2,1)} %weight_ref.3), custom_call_target="tpu_custom_call" | custom-call | flops 10116661248 | bytes 6422528 | tf_op jit(solution)/shard_map/attend/pallas_call | solution.py:189
  30.2 0.0 collective-permute-done.1.x1_ref
  30.2 0.0 collective-permute-done.2.x3_ref
  30.2 0.0 collective-permute-done.rest_2_
  30.3 0.1 collective-permute-start.4
  30.3 1.9 %collective-permute-start.5 = (bf16[2,104,1024]{2,1,0:T(8,128)(2,1)}, bf16[2,104,1024]{2,1,0:T(8,128)(2,1)}, u32[]{:S(2)}, u32[]{:S(2)}) collective-permute-start(bf16[2,104,1024]{2,1,0:T(8,128)(2,1)} %get-tuple-element.35), channel_id=1, source_target_pairs={{0,8},{4,12},{8,0},{12,4},{1,9},{5,13},{9,1},{13,5},{2,10},{6,14},... | collective-permute-start | bytes 1277960 | tf_op jit(solution)/shard_map/ppermute | solution.py:375
  32.2 1.3 collective-permute-start.7
  33.5 17.0 %attend.3 = bf16[16,2,112,256]{3,2,1,0:T(8,128)(2,1)} custom-call(bf16[2,1568,1024]{2,1,0:T(8,128)(2,1)} %x_ref.3, s32[2,16,128]{2,1,0:T(8,128)} %reshape.19.order_ref, f32[2,256]{1,0:T(2,128)} %decay_ref.3, s32[2]{0:T(128)} %clip_ref.3, bf16[3,1024,256]{2,1,0:T(8,128)(2,1)} %weight_ref.3, ...), custom_call_target="tpu_custom_call", output_to_operand_aliasing={{}: (5, {})} | custom-call | flops 10116661248 | bytes 6422528 | tf_op jit(solution)/shard_map/attend/pallas_call | solution.py:189
  50.6 0.0 collective-permute-done.5.x2_ref
  50.6 0.0 collective-permute-done.3.rest_3_
  50.6 0.0 collective-permute-done.4.rest_4_
  50.6 4.5 %all-to-all-start = ((bf16[16,2,112,256]{3,2,1,0:T(8,128)(2,1)}), bf16[16,2,112,256]{3,2,1,0:T(8,128)(2,1)S(1)}, u32[]{:S(2)}, u32[]{:S(2)}) async-start(bf16[16,2,112,256]{3,2,1,0:T(8,128)(2,1)} %attend.3), calls=%async_computation | async-start | bytes 3670016 | tf_op jit(solution)/shard_map/all_to_all | solution.py:389
  55.1 0.0 collective-permute-done.7.rest_6_
  55.1 0.1 collective-permute-start.8
  55.2 0.5 collective-permute-start.6
  55.7 2.7 %collective-permute-done.8.rest_7_ = bf16[2560,256]{1,0:T(8,128)(2,1)S(1)} collective-permute-done((bf16[2560,256]{1,0:T(8,128)(2,1)}, bf16[2560,256]{1,0:T(8,128)(2,1)S(1)}, u32[]{:S(2)}, u32[]{:S(2)}) %collective-permute-start.8) | collective-permute-done | bytes 1310752 | tf_op jit(solution)/shard_map/ppermute | solution.py:370
  58.5 2.0 %collective-permute-done.6.rest_5_ = bf16[2560,256]{1,0:T(8,128)(2,1)} collective-permute-done((bf16[2560,256]{1,0:T(8,128)(2,1)}, bf16[2560,256]{1,0:T(8,128)(2,1)}, u32[]{:S(2)}, u32[]{:S(2)}) %collective-permute-start.6) | collective-permute-done | bytes 1310752 | tf_op jit(solution)/shard_map/ppermute | solution.py:370
  60.5 22.0 %all-to-all-done.att_ref = bf16[16,2,112,256]{3,2,1,0:T(8,128)(2,1)S(1)} async-done(((bf16[16,2,112,256]{3,2,1,0:T(8,128)(2,1)}), bf16[16,2,112,256]{3,2,1,0:T(8,128)(2,1)S(1)}, u32[]{:S(2)}, u32[]{:S(2)}) %all-to-all-start) | async-done | bytes 1835040 | tf_op jit(solution)/shard_map/all_to_all | solution.py:389
  82.5 11.4 %recur.1 = (f32[4,208,1024]{2,1,0:T(8,128)S(1)}, f32[4,832,256]{2,1,0:T(8,128)S(1)}, f32[4,16,256]{2,1,0:T(8,128)S(1)}, f32[4,832,256]{2,1,0:T(8,128)S(1)}, bf16[4,112,256]{2,1,0:T(8,128)(2,1)S(1)}) custom-call(s32[3]{0:T(128)S(1)} %copy-done, bf16[16,2,112,256]{3,2,1,0:T(8,128)(2,1)S(1)} %all-to-all-done.att_ref, ...), custom_call_target="tpu_custom_call" | custom-call | tf_op jit(solution)/shard_map/recur/pallas_call | solution.py:393
  94.0 3.8 %collective-permute-start.9 = (bf16[4,112,256]{2,1,0:T(8,128)(2,1)S(1)}, bf16[4,112,256]{2,1,0:T(8,128)(2,1)S(1)}, u32[]{:S(2)}, u32[]{:S(2)}) collective-permute-start(bf16[4,112,256]{2,1,0:T(8,128)(2,1)S(1)} %get-tuple-element.47), channel_id=1, source_target_pairs={{0,16},{16,32},{32,48},{1,17},{17,33},{33,49},{2,18},{18,34},{34,5... | collective-permute-start | bytes 688136 | tf_op jit(solution)/shard_map/ppermute | solution.py:428
  97.8 4.1 %collective-permute-done.9.incoming_ref = bf16[4,112,256]{2,1,0:T(8,128)(2,1)S(1)} collective-permute-done((bf16[4,112,256]{2,1,0:T(8,128)(2,1)S(1)}, bf16[4,112,256]{2,1,0:T(8,128)(2,1)S(1)}, u32[]{:S(2)}, u32[]{:S(2)}) %collective-permute-start.9) | collective-permute-done | bytes 229408 | tf_op jit(solution)/shard_map/ppermute | solution.py:428
  101.9 5.0 %finish.1 = bf16[4,4,2,104,256]{4,3,2,1,0:T(8,128)(2,1)S(1)} custom-call(s32[3]{0:T(128)S(1)} %copy-done, f32[4,832,256]{2,1,0:T(8,128)S(1)} %get-tuple-element.44.state_ref, f32[4,16,256]{2,1,0:T(8,128)S(1)} %get-tuple-element.45.decay_ref, f32[4,832,256]{2,1,0:T(8,128)S(1)} %get-tuple-element.46.open_ref, ...), custom_call_target="tpu_custom_call" | custom-call | tf_op jit(solution)/shard_map/finish/pallas_call | solution.py:430
  106.9 24.6 %all_to_all.10 = bf16[16,2,104,256]{3,2,1,0:T(8,128)(2,1)} all-to-all(bf16[16,2,104,256]{3,2,1,0:T(8,128)(2,1)S(1)} %bitcast.7), channel_id=1, replica_groups=mesh['clip'=2,'z'=4,'x'=4,'head'=4] {'x','head'}, dimensions={0} | all-to-all | bytes 3407872 | tf_op jit(solution)/shard_map/all_to_all | solution.py:453
  131.5 2.4 %place.1 = bf16[2,4,392,256]{3,2,1,0:T(8,128)(2,1)} custom-call(bf16[4,4,2,104,256]{4,3,2,1,0:T(8,128)(2,1)} %bitcast.8), custom_call_target="tpu_custom_call" | custom-call | tf_op jit(solution)/shard_map/place/pallas_call | solution.py:454
  (9 shorter events, 0.0 us)
Async XLA Ops:
  0.6 11.7 %copy-start.3 = (s32[2,1568]{1,0:T(2,128)S(1)}, s32[2,1568]{1,0:T(2,128)}, u32[]{:S(2)}) copy-start(s32[2,1568]{1,0:T(2,128)} %param.9) | copy-start | bytes 37636
  5.9 24.4 %collective-permute-start = (bf16[2560,256]{1,0:T(8,128)(2,1)}, bf16[2560,256]{1,0:T(8,128)(2,1)S(1)}, u32[]{:S(2)}, u32[]{:S(2)}) collective-permute-start(bf16[2560,256]{1,0:T(8,128)(2,1)} %get-tuple-element.27.rest_0_), channel_id=1, source_target_pairs={{0,1},{1,2},{2,3},{3,0},{64,67},{65,64},{66,65},{67,66},{4,5},{5,6... | collective-permute-start | bytes 3932168 | tf_op jit(solution)/shard_map/ppermute | solution.py:367
  7.5 22.7 %collective-permute-start.1 = (bf16[2,104,1024]{2,1,0:T(8,128)(2,1)}, bf16[2,104,1024]{2,1,0:T(8,128)(2,1)}, u32[]{:S(2)}, u32[]{:S(2)}) collective-permute-start(bf16[2,104,1024]{2,1,0:T(8,128)(2,1)} %get-tuple-element.28), channel_id=1, source_target_pairs={{0,4},{4,8},{8,12},{12,0},{1,5},{5,9},{9,13},{13,1},{2,6},{6,10},{... | collective-permute-start | bytes 1277960 | tf_op jit(solution)/shard_map/ppermute | solution.py:375
  9.0 21.2 %collective-permute-start.2 = (bf16[2,104,1024]{2,1,0:T(8,128)(2,1)}, bf16[2,104,1024]{2,1,0:T(8,128)(2,1)}, u32[]{:S(2)}, u32[]{:S(2)}) collective-permute-start(bf16[2,104,1024]{2,1,0:T(8,128)(2,1)} %get-tuple-element.29), channel_id=1, source_target_pairs={{0,12},{4,0},{8,4},{12,8},{1,13},{5,1},{9,5},{13,9},{2,14},{6,2},{... | collective-permute-start | bytes 1277960 | tf_op jit(solution)/shard_map/ppermute | solution.py:375
  10.7 39.8 %collective-permute-start.3 = (bf16[2560,256]{1,0:T(8,128)(2,1)}, bf16[2560,256]{1,0:T(8,128)(2,1)}, u32[]{:S(2)}, u32[]{:S(2)}) collective-permute-start(bf16[2560,256]{1,0:T(8,128)(2,1)} %get-tuple-element.31.rest_1_), channel_id=1, source_target_pairs={{0,1},{1,2},{2,3},{3,0},{64,67},{65,64},{66,65},{67,66},{4,5},{5,6... | collective-permute-start | bytes 3932168 | tf_op jit(solution)/shard_map/ppermute | solution.py:367
  30.2 20.3 %copy-start.1 = (bf16[2560,256]{1,0:T(8,128)(2,1)}, bf16[2560,256]{1,0:T(8,128)(2,1)S(1)}, u32[]{:S(2)}) copy-start(bf16[2560,256]{1,0:T(8,128)(2,1)S(1)} %collective-permute-done.rest_2_) | copy-start | bytes 3932164
  30.3 20.4 %collective-permute-start.4 = (bf16[2560,256]{1,0:T(8,128)(2,1)S(1)}, bf16[2560,256]{1,0:T(8,128)(2,1)}, u32[]{:S(2)}, u32[]{:S(2)}) collective-permute-start(bf16[2560,256]{1,0:T(8,128)(2,1)S(1)} %collective-permute-done.rest_2_), channel_id=1, source_target_pairs={{0,64},{64,0},{1,65},{65,1},{2,66},{66,2},{3,67},{67,3},{4,68},{68... | collective-permute-start | bytes 3932168 | tf_op jit(solution)/shard_map/ppermute | solution.py:370
  30.3 20.2 %collective-permute-start.5 = (bf16[2,104,1024]{2,1,0:T(8,128)(2,1)}, bf16[2,104,1024]{2,1,0:T(8,128)(2,1)}, u32[]{:S(2)}, u32[]{:S(2)}) collective-permute-start(bf16[2,104,1024]{2,1,0:T(8,128)(2,1)} %get-tuple-element.35), channel_id=1, source_target_pairs={{0,8},{4,12},{8,0},{12,4},{1,9},{5,13},{9,1},{13,5},{2,10},{6,14},... | collective-permute-start | bytes 1277960 | tf_op jit(solution)/shard_map/ppermute | solution.py:375
  32.2 22.9 %collective-permute-start.7 = (bf16[2560,256]{1,0:T(8,128)(2,1)S(1)}, bf16[2560,256]{1,0:T(8,128)(2,1)}, u32[]{:S(2)}, u32[]{:S(2)}) collective-permute-start(bf16[2560,256]{1,0:T(8,128)(2,1)S(1)} %collective-permute-done.rest_2_), channel_id=1, source_target_pairs={{0,1},{1,2},{2,3},{3,0},{64,67},{65,64},{66,65},{67,66},{4,5},{5,6... | collective-permute-start | bytes 3932168 | tf_op jit(solution)/shard_map/ppermute | solution.py:367
  50.6 31.9 %copy-start = (s32[3]{0:T(128)S(1)}, s32[3]{0:T(128)}, u32[]{:S(2)}) copy-start(s32[3]{0:T(128)} %pad_add_fusion.place_ref) | copy-start | bytes 40
  50.6 31.9 %all-to-all-start = ((bf16[16,2,112,256]{3,2,1,0:T(8,128)(2,1)}), bf16[16,2,112,256]{3,2,1,0:T(8,128)(2,1)S(1)}, u32[]{:S(2)}, u32[]{:S(2)}) async-start(bf16[16,2,112,256]{3,2,1,0:T(8,128)(2,1)} %attend.3), calls=%async_computation | async-start | bytes 3670016 | tf_op jit(solution)/shard_map/all_to_all | solution.py:389
  55.1 3.3 %collective-permute-start.8 = (bf16[2560,256]{1,0:T(8,128)(2,1)}, bf16[2560,256]{1,0:T(8,128)(2,1)S(1)}, u32[]{:S(2)}, u32[]{:S(2)}) collective-permute-start(bf16[2560,256]{1,0:T(8,128)(2,1)} %collective-permute-done.7.rest_6_), channel_id=1, source_target_pairs={{0,64},{64,0},{1,65},{65,1},{2,66},{66,2},{3,67},{67,3},{4,68},{68... | collective-permute-start | bytes 3932168 | tf_op jit(solution)/shard_map/ppermute | solution.py:370
  55.2 5.2 %collective-permute-start.6 = (bf16[2560,256]{1,0:T(8,128)(2,1)}, bf16[2560,256]{1,0:T(8,128)(2,1)}, u32[]{:S(2)}, u32[]{:S(2)}) collective-permute-start(bf16[2560,256]{1,0:T(8,128)(2,1)} %collective-permute-done.3.rest_3_), channel_id=1, source_target_pairs={{0,64},{64,0},{1,65},{65,1},{2,66},{66,2},{3,67},{67,3},{4,68},{68... | collective-permute-start | bytes 3932168 | tf_op jit(solution)/shard_map/ppermute | solution.py:370
  58.5 24.1 %copy-start.2 = (bf16[2560,256]{1,0:T(8,128)(2,1)}, bf16[2560,256]{1,0:T(8,128)(2,1)S(1)}, u32[]{:S(2)}) copy-start(bf16[2560,256]{1,0:T(8,128)(2,1)S(1)} %collective-permute-done.8.rest_7_) | copy-start | bytes 3932164
  94.0 7.9 %collective-permute-start.9 = (bf16[4,112,256]{2,1,0:T(8,128)(2,1)S(1)}, bf16[4,112,256]{2,1,0:T(8,128)(2,1)S(1)}, u32[]{:S(2)}, u32[]{:S(2)}) collective-permute-start(bf16[4,112,256]{2,1,0:T(8,128)(2,1)S(1)} %get-tuple-element.47), channel_id=1, source_target_pairs={{0,16},{16,32},{32,48},{1,17},{17,33},{33,49},{2,18},{18,34},{34,5... | collective-permute-start | bytes 688136 | tf_op jit(solution)/shard_map/ppermute | solution.py:428

commit v5 on v4

--- a/solution.py
+++ b/solution.py
@@ -114,7 +114,7 @@
     row_index = lax.broadcasted_iota(jnp.int32, (C, C), 0)
     lane_index = lax.broadcasted_iota(jnp.int32, (C, C), 1)
     together = jnp.where(row_index // HEAD == lane_index // HEAD, 1.0, 0.0).astype(BF16)
-    group = 16
+    group = 32
     lane = lax.broadcasted_iota(jnp.int32, (group * SLOT, 128), 1)
     low = lane < SLOT
     valid = (lane % SLOT) < WINDOW

time: 135 us -> 134 us (level)
  no operation moved by 1% of the time
where the time goes in v5:
time: 134 us; the launch traced here: 133 us
  Pallas kernels  57.5 us (43%)
  waiting for transfers between devices  30.8 us (23%)
  blocking collectives  24.6 us (18%)
  starting transfers between devices  18.7 us (14%)
    pallas_call x2, Pallas kernels, attend(): pl.pallas_call(functools.partial(attend_kernel, f), grid=(1,), in_specs=[...  33.4 us
    all_to_all x1, blocking collectives, per_device(): lax.all_to_all(result.reshape(16, FRAMES, SHARE, C), ('x', 'head'), 0, 0)  24.6 us
    all_to_all x1, waiting for transfers between devices, per_device(): mixed = lax.all_to_all(mixed, ('x', 'head'), 0, 0)  22 us
    pallas_call x1, Pallas kernels, per_device(): pl.pallas_call(recur_kernel, grid=(4,), in_specs=[pl.BlockSpec(memory_spa...  11.4 us
    pallas_call x1, Pallas kernels, per_device(): pl.pallas_call(pack_kernel, in_specs=[pl.BlockSpec(memory_space=pltpu.SME...  5.27 us
    ppermute x3, starting transfers between devices, per_device(): lax.ppermute(blocks[s], 'x', [(i, (i + s) % 4) for i in range(4)])  5.14 us
    pallas_call x1, Pallas kernels, per_device(): pl.pallas_call(finish_kernel, grid=(4,), in_specs=[pl.BlockSpec(memory_sp...  5.03 us
    ppermute x3, waiting for transfers between devices, across(): return lax.ppermute(value, 'clip', [(0, 1), (1, 0)])  4.74 us
  transfers between devices with their start and end apart: 11, of which 4 were waited for; matrix products, arithmetic and copies ran while one was open for 1% of the time, Pallas kernels for 25%

profile of v5, /device:TPU:32, one launch (start us, length us, event | category | flops | bytes accessed | tf_op | source)
XLA Modules:
  0.0 133.3 jit_solution(11462964609652917213)
XLA Ops:
  0.0 0.6 pad_add_fusion.place_ref
  0.6 5.3 %pack.1 = (bf16[2560,256]{1,0:T(8,128)(2,1)}, bf16[2560,256]{1,0:T(8,128)(2,1)}, bf16[2,104,1024]{2,1,0:T(8,128)(2,1)}, bf16[2,104,1024]{2,1,0:T(8,128)(2,1)}, b...) custom-call(s32[3]{0:T(128)} %pad_add_fusion.place_ref, bf16[2,4,392,1024]{3,2,1,0:T(8,128)(2,1)} %bitcast.9, ...), custom_call_target="tpu_custom_call" | custom-call | tf_op jit(solution)/shard_map/pack/pallas_call | solution.py:348
  5.9 1.6 %collective-permute-start = (bf16[2560,256]{1,0:T(8,128)(2,1)}, bf16[2560,256]{1,0:T(8,128)(2,1)S(1)}, u32[]{:S(2)}, u32[]{:S(2)}) collective-permute-start(bf16[2560,256]{1,0:T(8,128)(2,1)} %get-tuple-element.27.rest_0_), channel_id=1, source_target_pairs={{0,1},{1,2},{2,3},{3,0},{64,67},{65,64},{66,65},{67,66},{4,5},{5,6... | collective-permute-start | bytes 3932168 | tf_op jit(solution)/shard_map/ppermute | solution.py:367
  7.5 1.5 %collective-permute-start.1 = (bf16[2,104,1024]{2,1,0:T(8,128)(2,1)}, bf16[2,104,1024]{2,1,0:T(8,128)(2,1)}, u32[]{:S(2)}, u32[]{:S(2)}) collective-permute-start(bf16[2,104,1024]{2,1,0:T(8,128)(2,1)} %get-tuple-element.28), channel_id=1, source_target_pairs={{0,4},{4,8},{8,12},{12,0},{1,5},{5,9},{9,13},{13,1},{2,6},{6,10},{... | collective-permute-start | bytes 1277960 | tf_op jit(solution)/shard_map/ppermute | solution.py:375
  9.0 1.7 %collective-permute-start.2 = (bf16[2,104,1024]{2,1,0:T(8,128)(2,1)}, bf16[2,104,1024]{2,1,0:T(8,128)(2,1)}, u32[]{:S(2)}, u32[]{:S(2)}) collective-permute-start(bf16[2,104,1024]{2,1,0:T(8,128)(2,1)} %get-tuple-element.29), channel_id=1, source_target_pairs={{0,12},{4,0},{8,4},{12,8},{1,13},{5,1},{9,5},{13,9},{2,14},{6,2},{... | collective-permute-start | bytes 1277960 | tf_op jit(solution)/shard_map/ppermute | solution.py:375
  10.7 1.6 %collective-permute-start.3 = (bf16[2560,256]{1,0:T(8,128)(2,1)}, bf16[2560,256]{1,0:T(8,128)(2,1)}, u32[]{:S(2)}, u32[]{:S(2)}) collective-permute-start(bf16[2560,256]{1,0:T(8,128)(2,1)} %get-tuple-element.31.rest_1_), channel_id=1, source_target_pairs={{0,1},{1,2},{2,3},{3,0},{64,67},{65,64},{66,65},{67,66},{4,5},{5,6... | collective-permute-start | bytes 3932168 | tf_op jit(solution)/shard_map/ppermute | solution.py:367
  12.3 0.1 reshape.18
  12.5 0.7 reshape.19.order_ref
  13.1 16.7 %attend.2.rest_0_ = bf16[16,2,112,256]{3,2,1,0:T(8,128)(2,1)} custom-call(bf16[2,1568,1024]{2,1,0:T(8,128)(2,1)} %x_ref.3, s32[2,16,128]{2,1,0:T(8,128)} %reshape.19.order_ref, f32[2,256]{1,0:T(2,128)} %decay_ref.3, s32[2]{0:T(128)} %clip_ref.3, bf16[3,1024,256]{2,1,0:T(8,128)(2,1)} %weight_ref.3), custom_call_target="tpu_custom_call" | custom-call | flops 10116661248 | bytes 6422528 | tf_op jit(solution)/shard_map/attend/pallas_call | solution.py:189
  29.8 0.0 collective-permute-done.1.x1_ref
  29.9 0.0 collective-permute-done.2.x3_ref
  29.9 0.0 collective-permute-done.rest_2_
  29.9 0.1 collective-permute-start.4
  30.0 1.9 %collective-permute-start.5 = (bf16[2,104,1024]{2,1,0:T(8,128)(2,1)}, bf16[2,104,1024]{2,1,0:T(8,128)(2,1)}, u32[]{:S(2)}, u32[]{:S(2)}) collective-permute-start(bf16[2,104,1024]{2,1,0:T(8,128)(2,1)} %get-tuple-element.35), channel_id=1, source_target_pairs={{0,8},{4,12},{8,0},{12,4},{1,9},{5,13},{9,1},{13,5},{2,10},{6,14},... | collective-permute-start | bytes 1277960 | tf_op jit(solution)/shard_map/ppermute | solution.py:375
  31.9 1.3 collective-permute-start.7
  33.2 16.7 %attend.3 = bf16[16,2,112,256]{3,2,1,0:T(8,128)(2,1)} custom-call(bf16[2,1568,1024]{2,1,0:T(8,128)(2,1)} %x_ref.3, s32[2,16,128]{2,1,0:T(8,128)} %reshape.19.order_ref, f32[2,256]{1,0:T(2,128)} %decay_ref.3, s32[2]{0:T(128)} %clip_ref.3, bf16[3,1024,256]{2,1,0:T(8,128)(2,1)} %weight_ref.3, ...), custom_call_target="tpu_custom_call", output_to_operand_aliasing={{}: (5, {})} | custom-call | flops 10116661248 | bytes 6422528 | tf_op jit(solution)/shard_map/attend/pallas_call | solution.py:189
  49.9 0.0 collective-permute-done.5.x2_ref
  49.9 0.0 collective-permute-done.3.rest_3_
  49.9 0.0 collective-permute-done.4.rest_4_
  49.9 4.5 %all-to-all-start = ((bf16[16,2,112,256]{3,2,1,0:T(8,128)(2,1)}), bf16[16,2,112,256]{3,2,1,0:T(8,128)(2,1)S(1)}, u32[]{:S(2)}, u32[]{:S(2)}) async-start(bf16[16,2,112,256]{3,2,1,0:T(8,128)(2,1)} %attend.3), calls=%async_computation | async-start | bytes 3670016 | tf_op jit(solution)/shard_map/all_to_all | solution.py:389
  54.4 0.0 collective-permute-done.7.rest_6_
  54.4 0.1 collective-permute-start.8
  54.5 0.5 collective-permute-start.6
  55.0 2.7 %collective-permute-done.8.rest_7_ = bf16[2560,256]{1,0:T(8,128)(2,1)S(1)} collective-permute-done((bf16[2560,256]{1,0:T(8,128)(2,1)}, bf16[2560,256]{1,0:T(8,128)(2,1)S(1)}, u32[]{:S(2)}, u32[]{:S(2)}) %collective-permute-start.8) | collective-permute-done | bytes 1310752 | tf_op jit(solution)/shard_map/ppermute | solution.py:370
  57.8 2.0 %collective-permute-done.6.rest_5_ = bf16[2560,256]{1,0:T(8,128)(2,1)} collective-permute-done((bf16[2560,256]{1,0:T(8,128)(2,1)}, bf16[2560,256]{1,0:T(8,128)(2,1)}, u32[]{:S(2)}, u32[]{:S(2)}) %collective-permute-start.6) | collective-permute-done | bytes 1310752 | tf_op jit(solution)/shard_map/ppermute | solution.py:370
  59.8 22.0 %all-to-all-done.att_ref = bf16[16,2,112,256]{3,2,1,0:T(8,128)(2,1)S(1)} async-done(((bf16[16,2,112,256]{3,2,1,0:T(8,128)(2,1)}), bf16[16,2,112,256]{3,2,1,0:T(8,128)(2,1)S(1)}, u32[]{:S(2)}, u32[]{:S(2)}) %all-to-all-start) | async-done | bytes 1835040 | tf_op jit(solution)/shard_map/all_to_all | solution.py:389
  81.8 11.4 %recur.1 = (f32[4,208,1024]{2,1,0:T(8,128)S(1)}, f32[4,832,256]{2,1,0:T(8,128)S(1)}, f32[4,16,256]{2,1,0:T(8,128)S(1)}, f32[4,832,256]{2,1,0:T(8,128)S(1)}, bf16[4,112,256]{2,1,0:T(8,128)(2,1)S(1)}) custom-call(s32[3]{0:T(128)S(1)} %copy-done, bf16[16,2,112,256]{3,2,1,0:T(8,128)(2,1)S(1)} %all-to-all-done.att_ref, ...), custom_call_target="tpu_custom_call" | custom-call | tf_op jit(solution)/shard_map/recur/pallas_call | solution.py:393
  93.2 3.9 %collective-permute-start.9 = (bf16[4,112,256]{2,1,0:T(8,128)(2,1)S(1)}, bf16[4,112,256]{2,1,0:T(8,128)(2,1)S(1)}, u32[]{:S(2)}, u32[]{:S(2)}) collective-permute-start(bf16[4,112,256]{2,1,0:T(8,128)(2,1)S(1)} %get-tuple-element.47), channel_id=1, source_target_pairs={{0,16},{16,32},{32,48},{1,17},{17,33},{33,49},{2,18},{18,34},{34,5... | collective-permute-start | bytes 688136 | tf_op jit(solution)/shard_map/ppermute | solution.py:428
  97.1 4.1 %collective-permute-done.9.incoming_ref = bf16[4,112,256]{2,1,0:T(8,128)(2,1)S(1)} collective-permute-done((bf16[4,112,256]{2,1,0:T(8,128)(2,1)S(1)}, bf16[4,112,256]{2,1,0:T(8,128)(2,1)S(1)}, u32[]{:S(2)}, u32[]{:S(2)}) %collective-permute-start.9) | collective-permute-done | bytes 229408 | tf_op jit(solution)/shard_map/ppermute | solution.py:428
  101.1 5.0 %finish.1 = bf16[4,4,2,104,256]{4,3,2,1,0:T(8,128)(2,1)S(1)} custom-call(s32[3]{0:T(128)S(1)} %copy-done, f32[4,832,256]{2,1,0:T(8,128)S(1)} %get-tuple-element.44.state_ref, f32[4,16,256]{2,1,0:T(8,128)S(1)} %get-tuple-element.45.decay_ref, f32[4,832,256]{2,1,0:T(8,128)S(1)} %get-tuple-element.46.open_ref, ...), custom_call_target="tpu_custom_call" | custom-call | tf_op jit(solution)/shard_map/finish/pallas_call | solution.py:430
  106.1 24.6 %all_to_all.10 = bf16[16,2,104,256]{3,2,1,0:T(8,128)(2,1)} all-to-all(bf16[16,2,104,256]{3,2,1,0:T(8,128)(2,1)S(1)} %bitcast.7), channel_id=1, replica_groups=mesh['clip'=2,'z'=4,'x'=4,'head'=4] {'x','head'}, dimensions={0} | all-to-all | bytes 3407872 | tf_op jit(solution)/shard_map/all_to_all | solution.py:453
  130.7 2.4 %place.1 = bf16[2,4,392,256]{3,2,1,0:T(8,128)(2,1)} custom-call(bf16[4,4,2,104,256]{4,3,2,1,0:T(8,128)(2,1)} %bitcast.8), custom_call_target="tpu_custom_call" | custom-call | tf_op jit(solution)/shard_map/place/pallas_call | solution.py:454
  (9 shorter events, 0.0 us)
Async XLA Ops:
  0.6 11.7 %copy-start.3 = (s32[2,1568]{1,0:T(2,128)S(1)}, s32[2,1568]{1,0:T(2,128)}, u32[]{:S(2)}) copy-start(s32[2,1568]{1,0:T(2,128)} %param.9) | copy-start | bytes 37636
  5.9 24.0 %collective-permute-start = (bf16[2560,256]{1,0:T(8,128)(2,1)}, bf16[2560,256]{1,0:T(8,128)(2,1)S(1)}, u32[]{:S(2)}, u32[]{:S(2)}) collective-permute-start(bf16[2560,256]{1,0:T(8,128)(2,1)} %get-tuple-element.27.rest_0_), channel_id=1, source_target_pairs={{0,1},{1,2},{2,3},{3,0},{64,67},{65,64},{66,65},{67,66},{4,5},{5,6... | collective-permute-start | bytes 3932168 | tf_op jit(solution)/shard_map/ppermute | solution.py:367
  7.5 22.3 %collective-permute-start.1 = (bf16[2,104,1024]{2,1,0:T(8,128)(2,1)}, bf16[2,104,1024]{2,1,0:T(8,128)(2,1)}, u32[]{:S(2)}, u32[]{:S(2)}) collective-permute-start(bf16[2,104,1024]{2,1,0:T(8,128)(2,1)} %get-tuple-element.28), channel_id=1, source_target_pairs={{0,4},{4,8},{8,12},{12,0},{1,5},{5,9},{9,13},{13,1},{2,6},{6,10},{... | collective-permute-start | bytes 1277960 | tf_op jit(solution)/shard_map/ppermute | solution.py:375
  9.0 20.9 %collective-permute-start.2 = (bf16[2,104,1024]{2,1,0:T(8,128)(2,1)}, bf16[2,104,1024]{2,1,0:T(8,128)(2,1)}, u32[]{:S(2)}, u32[]{:S(2)}) collective-permute-start(bf16[2,104,1024]{2,1,0:T(8,128)(2,1)} %get-tuple-element.29), channel_id=1, source_target_pairs={{0,12},{4,0},{8,4},{12,8},{1,13},{5,1},{9,5},{13,9},{2,14},{6,2},{... | collective-permute-start | bytes 1277960 | tf_op jit(solution)/shard_map/ppermute | solution.py:375
  10.7 39.1 %collective-permute-start.3 = (bf16[2560,256]{1,0:T(8,128)(2,1)}, bf16[2560,256]{1,0:T(8,128)(2,1)}, u32[]{:S(2)}, u32[]{:S(2)}) collective-permute-start(bf16[2560,256]{1,0:T(8,128)(2,1)} %get-tuple-element.31.rest_1_), channel_id=1, source_target_pairs={{0,1},{1,2},{2,3},{3,0},{64,67},{65,64},{66,65},{67,66},{4,5},{5,6... | collective-permute-start | bytes 3932168 | tf_op jit(solution)/shard_map/ppermute | solution.py:367
  29.9 20.0 %copy-start.1 = (bf16[2560,256]{1,0:T(8,128)(2,1)}, bf16[2560,256]{1,0:T(8,128)(2,1)S(1)}, u32[]{:S(2)}) copy-start(bf16[2560,256]{1,0:T(8,128)(2,1)S(1)} %collective-permute-done.rest_2_) | copy-start | bytes 3932164
  29.9 20.0 %collective-permute-start.4 = (bf16[2560,256]{1,0:T(8,128)(2,1)S(1)}, bf16[2560,256]{1,0:T(8,128)(2,1)}, u32[]{:S(2)}, u32[]{:S(2)}) collective-permute-start(bf16[2560,256]{1,0:T(8,128)(2,1)S(1)} %collective-permute-done.rest_2_), channel_id=1, source_target_pairs={{0,64},{64,0},{1,65},{65,1},{2,66},{66,2},{3,67},{67,3},{4,68},{68... | collective-permute-start | bytes 3932168 | tf_op jit(solution)/shard_map/ppermute | solution.py:370
  30.0 19.9 %collective-permute-start.5 = (bf16[2,104,1024]{2,1,0:T(8,128)(2,1)}, bf16[2,104,1024]{2,1,0:T(8,128)(2,1)}, u32[]{:S(2)}, u32[]{:S(2)}) collective-permute-start(bf16[2,104,1024]{2,1,0:T(8,128)(2,1)} %get-tuple-element.35), channel_id=1, source_target_pairs={{0,8},{4,12},{8,0},{12,4},{1,9},{5,13},{9,1},{13,5},{2,10},{6,14},... | collective-permute-start | bytes 1277960 | tf_op jit(solution)/shard_map/ppermute | solution.py:375
  31.9 22.5 %collective-permute-start.7 = (bf16[2560,256]{1,0:T(8,128)(2,1)S(1)}, bf16[2560,256]{1,0:T(8,128)(2,1)}, u32[]{:S(2)}, u32[]{:S(2)}) collective-permute-start(bf16[2560,256]{1,0:T(8,128)(2,1)S(1)} %collective-permute-done.rest_2_), channel_id=1, source_target_pairs={{0,1},{1,2},{2,3},{3,0},{64,67},{65,64},{66,65},{67,66},{4,5},{5,6... | collective-permute-start | bytes 3932168 | tf_op jit(solution)/shard_map/ppermute | solution.py:367
  49.9 31.9 %copy-start = (s32[3]{0:T(128)S(1)}, s32[3]{0:T(128)}, u32[]{:S(2)}) copy-start(s32[3]{0:T(128)} %pad_add_fusion.place_ref) | copy-start | bytes 40
  49.9 31.9 %all-to-all-start = ((bf16[16,2,112,256]{3,2,1,0:T(8,128)(2,1)}), bf16[16,2,112,256]{3,2,1,0:T(8,128)(2,1)S(1)}, u32[]{:S(2)}, u32[]{:S(2)}) async-start(bf16[16,2,112,256]{3,2,1,0:T(8,128)(2,1)} %attend.3), calls=%async_computation | async-start | bytes 3670016 | tf_op jit(solution)/shard_map/all_to_all | solution.py:389
  54.4 3.3 %collective-permute-start.8 = (bf16[2560,256]{1,0:T(8,128)(2,1)}, bf16[2560,256]{1,0:T(8,128)(2,1)S(1)}, u32[]{:S(2)}, u32[]{:S(2)}) collective-permute-start(bf16[2560,256]{1,0:T(8,128)(2,1)} %collective-permute-done.7.rest_6_), channel_id=1, source_target_pairs={{0,64},{64,0},{1,65},{65,1},{2,66},{66,2},{3,67},{67,3},{4,68},{68... | collective-permute-start | bytes 3932168 | tf_op jit(solution)/shard_map/ppermute | solution.py:370
  54.5 5.2 %collective-permute-start.6 = (bf16[2560,256]{1,0:T(8,128)(2,1)}, bf16[2560,256]{1,0:T(8,128)(2,1)}, u32[]{:S(2)}, u32[]{:S(2)}) collective-permute-start(bf16[2560,256]{1,0:T(8,128)(2,1)} %collective-permute-done.3.rest_3_), channel_id=1, source_target_pairs={{0,64},{64,0},{1,65},{65,1},{2,66},{66,2},{3,67},{67,3},{4,68},{68... | collective-permute-start | bytes 3932168 | tf_op jit(solution)/shard_map/ppermute | solution.py:370
  57.8 24.0 %copy-start.2 = (bf16[2560,256]{1,0:T(8,128)(2,1)}, bf16[2560,256]{1,0:T(8,128)(2,1)S(1)}, u32[]{:S(2)}) copy-start(bf16[2560,256]{1,0:T(8,128)(2,1)S(1)} %collective-permute-done.8.rest_7_) | copy-start | bytes 3932164
  93.2 7.9 %collective-permute-start.9 = (bf16[4,112,256]{2,1,0:T(8,128)(2,1)S(1)}, bf16[4,112,256]{2,1,0:T(8,128)(2,1)S(1)}, u32[]{:S(2)}, u32[]{:S(2)}) collective-permute-start(bf16[4,112,256]{2,1,0:T(8,128)(2,1)S(1)} %get-tuple-element.47), channel_id=1, source_target_pairs={{0,16},{16,32},{32,48},{1,17},{17,33},{33,49},{2,18},{18,34},{34,5... | collective-permute-start | bytes 688136 | tf_op jit(solution)/shard_map/ppermute | solution.py:428
